TPU v7x, 128 devices: a whole 4x4x4 slice. The times are simulated.
128 devices in a mesh: section: 2 (over z_lo), dp: 16 (over y, x), tensor: 4 (over z_hi, core).
Axes of the slice: x: 4, y: 4, z: 4 (z_hi: 2, z_lo: 2; z = z_hi * 2 + z_lo), core: 2. Of those that a mesh axis runs over, the one named last changes fastest.
Arguments:
- images: bfloat16 [48, 577, 768], P('dp', None, 'tensor'), may hold values from -6 to 6
- slot_table: int32 [32], P('dp'), may hold values from 0 to 3, as said below
- ln1_gain: float32 [2, 768], P('section'), may hold values from 0.5 to 1.5
- ln1_bias: float32 [2, 768], P('section'), may hold values from -1.5 to 1.5
- qkv_weight: bfloat16 [2, 768, 3, 768], P('section', None, None, 'tensor'), may hold values from -0.21875 to 0.21875
- qv_bias: float32 [2, 2, 768], P('section', None, 'tensor'), may hold values from -1.5 to 1.5
- out_weight: bfloat16 [2, 768, 768], P('section', 'tensor'), may hold values from -0.875 to 0.875
- out_bias: float32 [2, 768], P('section'), may hold values from -1.5 to 1.5
- ln2_gain: float32 [2, 768], P('section'), may hold values from 0.5 to 1.5
- ln2_bias: float32 [2, 768], P('section'), may hold values from -1.5 to 1.5
- fc1_weight: bfloat16 [2, 768, 3072], P('section', None, 'tensor'), may hold values from -0.21875 to 0.21875
- fc1_bias: float32 [2, 3072], P('section', 'tensor'), may hold values from -1.5 to 1.5
- fc2_weight: bfloat16 [2, 3072, 768], P('section', 'tensor'), may hold values from -0.109375 to 0.109375
- fc2_bias: float32 [2, 768], P('section'), may hold values from -1.5 to 1.5
- cotangent: bfloat16 [48, 577, 768], P('dp', None, 'tensor'), may hold values from -6 to 6
Outputs:
- activations: bfloat16 [2, 48, 577, 768], P('section', 'dp', None, 'tensor')
- input_grads: float32 [2, 48, 577, 768], P('section', 'dp', None, 'tensor')
- ln1_gain_grad: float32 [2, 768], P('section', 'tensor')
- ln1_bias_grad: float32 [2, 768], P('section', 'tensor')
- qkv_weight_grad: float32 [2, 768, 3, 768], P('section', None, None, 'tensor')
- qv_bias_grad: float32 [2, 2, 768], P('section', None, 'tensor')
- out_weight_grad: float32 [2, 768, 768], P('section', 'tensor')
- out_bias_grad: float32 [2, 768], P('section', 'tensor')
- ln2_gain_grad: float32 [2, 768], P('section', 'tensor')
- ln2_bias_grad: float32 [2, 768], P('section', 'tensor')
- fc1_weight_grad: float32 [2, 768, 3072], P('section', None, 'tensor')
- fc1_bias_grad: float32 [2, 3072], P('section', 'tensor')
- fc2_weight_grad: float32 [2, 3072, 768], P('section', 'tensor')
- fc2_bias_grad: float32 [2, 768], P('section', 'tensor')
Inputs may be any that keep to these rules, and one draw needn't show every extreme that they name: `slot_table`: within one data member's 2 entries, values below 3 are distinct; the value 3 means that the micro-batch has no image there.
All inputs are finite; a program needn't handle non-finite values.
Results may differ from a plain program's by a relative error of at most 0.0095.
Values may be sent and summed in bfloat16 or wider, within the bound.
No kernel may reach another device: no remote copies, remote signals or barrier semaphores. Data moves between devices by JAX's collectives and lax.ppermute only.
A program may use at most 192 MiB of HBM per device.

v0:
```python
from functools import partial

import jax
import jax.numpy as jnp
from jax import lax
from jax.sharding import PartitionSpec as P

HD = 64


epsilon = 1e-06


def shifted(block, axis, distance):
    devices = range(lax.axis_size(axis))
    route = [(i - distance, i) for i in devices if i - distance in devices]
    return lax.ppermute(block, axis, route)


def standardize_rows(values):
    row_means = jnp.mean(values, axis=1, keepdims=True)
    center = values - row_means
    inverse = lax.rsqrt(jnp.mean(center * center, axis=1, keepdims=True) + epsilon)
    return (center * inverse, row_means, inverse)


def contract_rows(left_side, right_side):
    return lax.dot_general(
        left_side, right_side, (((0,), (0,)), ((), ())), preferred_element_type=jnp.float32
    )


def contract_cols(left_side, right_side):
    return lax.dot_general(
        left_side, right_side, (((1,), (1,)), ((), ())), preferred_element_type=jnp.float32
    )


def member_sum(gradients):
    return lax.psum(gradients, "dp")


def layer_forward(partial_residual, params, column):
    (
        first_norm_gain,
        first_norm_bias,
        qkv_mat,
        qv_add,
        out_mat,
        out_add,
        second_norm_gain,
        second_norm_bias,
        up_mat,
        up_add,
        down_mat,
        down_add,
    ) = params
    rows_count = partial_residual.shape[0]
    part_width = partial_residual.shape[1]
    hidden_width = first_norm_gain.shape[0]
    head_count = part_width // HD

    def local_part(vector):
        return lax.dynamic_slice_in_dim(vector, column, part_width, 0)

    complete_residual = lax.all_gather(partial_residual, "tensor", axis=1, tiled=True)
    first_centered_unit, first_row_averages, first_inverse_deviation = standardize_rows(
        complete_residual.astype(jnp.float32)
    )
    first_normalized = (first_centered_unit * first_norm_gain + first_norm_bias).astype(
        jnp.bfloat16
    )
    projected = jnp.dot(
        first_normalized,
        qkv_mat.reshape(hidden_width, 3 * part_width),
        preferred_element_type=jnp.float32,
    ).reshape(rows_count, 3, part_width)
    queries = (projected[:, 0] + qv_add[0]).astype(jnp.bfloat16).reshape(rows_count, head_count, HD)
    keys_part = projected[:, 1].astype(jnp.bfloat16).reshape(rows_count, head_count, HD)
    values_part = (
        (projected[:, 2] + qv_add[1]).astype(jnp.bfloat16).reshape(rows_count, head_count, HD)
    )
    scores = jnp.einsum(
        "qhd,khd->hqk", queries, keys_part, preferred_element_type=jnp.float32
    ) * HD ** (-0.5)
    totals = jax.nn.logsumexp(scores, axis=2, keepdims=True)
    probabilities = jnp.exp(scores - totals)
    attended = (
        jnp.einsum(
            "hqk,khd->qhd",
            probabilities.astype(jnp.bfloat16),
            values_part,
            preferred_element_type=jnp.float32,
        )
        .reshape(rows_count, part_width)
        .astype(jnp.bfloat16)
    )
    branch = lax.psum_scatter(
        jnp.dot(attended, out_mat, preferred_element_type=jnp.float32),
        "tensor",
        scatter_dimension=1,
        tiled=True,
    )
    middle = partial_residual.astype(jnp.float32) + branch + local_part(out_add)
    complete_middle_state = lax.all_gather(
        middle.astype(jnp.bfloat16), "tensor", axis=1, tiled=True
    )
    second_centered_unit, second_row_averages, second_inverse_deviation = standardize_rows(
        complete_middle_state.astype(jnp.float32)
    )
    second_normalized = (second_centered_unit * second_norm_gain + second_norm_bias).astype(
        jnp.bfloat16
    )
    hidden_pre = jnp.dot(second_normalized, up_mat, preferred_element_type=jnp.float32) + up_add
    hidden = jax.nn.gelu(hidden_pre, approximate=False).astype(jnp.bfloat16)
    feed_out = lax.psum_scatter(
        jnp.dot(hidden, down_mat, preferred_element_type=jnp.float32),
        "tensor",
        scatter_dimension=1,
        tiled=True,
    )
    result = middle + feed_out + local_part(down_add)
    saved_state = (
        partial_residual,
        first_row_averages,
        first_inverse_deviation,
        first_normalized,
        queries,
        keys_part,
        values_part,
        totals,
        attended,
        complete_middle_state,
        second_row_averages,
        second_inverse_deviation,
        second_normalized,
        hidden_pre,
        hidden,
    )
    return (result.astype(jnp.bfloat16), saved_state)


def layer_backward(grad_part, saved_state, params, column, grad_sums):
    (
        first_norm_gain,
        first_norm_bias,
        qkv_mat,
        qv_add,
        out_mat,
        out_add,
        second_norm_gain,
        second_norm_bias,
        up_mat,
        up_add,
        down_mat,
        down_add,
    ) = params
    (
        partial_residual,
        first_row_averages,
        first_inverse_deviation,
        first_normalized,
        queries,
        keys_part,
        values_part,
        totals,
        attended,
        complete_middle_state,
        second_row_averages,
        second_inverse_deviation,
        second_normalized,
        hidden_pre,
        hidden,
    ) = saved_state
    rows_count = grad_part.shape[0]
    part_width = grad_part.shape[1]
    hidden_width = first_norm_gain.shape[0]
    head_count = part_width // HD

    def local_part(vector):
        return lax.dynamic_slice_in_dim(vector, column, part_width, 0)

    grad_full = lax.all_gather(grad_part.astype(jnp.bfloat16), "tensor", axis=1, tiled=True)
    down_grad = contract_rows(hidden, grad_full)
    down_add_grad = jnp.sum(grad_part, axis=0)
    hidden_grad = contract_cols(grad_full, down_mat)
    unused_value, gelu_back = jax.vjp(partial(jax.nn.gelu, approximate=False), hidden_pre)
    pre_grad = gelu_back(hidden_grad)[0].astype(jnp.bfloat16)
    up_grad = contract_rows(second_normalized, pre_grad)
    up_add_grad = jnp.sum(pre_grad.astype(jnp.float32), axis=0)
    normalized_gradient = lax.psum_scatter(
        contract_cols(pre_grad, up_mat), "tensor", scatter_dimension=1, tiled=True
    )
    local_middle_state = lax.dynamic_slice_in_dim(
        complete_middle_state, column, part_width, 1
    ).astype(jnp.float32)
    second_centered_unit = (local_middle_state - second_row_averages) * second_inverse_deviation
    second_gain_gradient = jnp.sum(normalized_gradient * second_centered_unit, axis=0)
    bias_two_grad = jnp.sum(normalized_gradient, axis=0)
    second_rescaled = normalized_gradient * local_part(second_norm_gain)
    first_running_total, second_running_total = lax.psum(
        (
            jnp.sum(second_rescaled, axis=1, keepdims=True),
            jnp.sum(second_rescaled * second_centered_unit, axis=1, keepdims=True),
        ),
        "tensor",
    )
    middle_grad = grad_part + second_inverse_deviation * (
        second_rescaled
        - first_running_total / hidden_width
        - second_centered_unit * second_running_total / hidden_width
    )
    feed_grads = (
        second_gain_gradient,
        bias_two_grad,
        up_grad,
        up_add_grad,
        down_grad,
        down_add_grad,
    )
    feed_grads = tuple((older + newer for older, newer in zip(grad_sums[6:], feed_grads)))
    branch_grad = lax.all_gather(middle_grad.astype(jnp.bfloat16), "tensor", axis=1, tiled=True)
    out_grad = contract_rows(attended, branch_grad)
    out_add_grad = jnp.sum(middle_grad, axis=0)
    attended_grad = (
        contract_cols(branch_grad, out_mat).astype(jnp.bfloat16).reshape(rows_count, head_count, HD)
    )
    scale_factor = HD ** (-0.5)
    scores = (
        jnp.einsum("qhd,khd->hqk", queries, keys_part, preferred_element_type=jnp.float32)
        * scale_factor
    )
    probabilities = jnp.exp(scores - totals)
    values_grad = jnp.einsum(
        "hqk,qhd->khd",
        probabilities.astype(jnp.bfloat16),
        attended_grad,
        preferred_element_type=jnp.float32,
    )
    weight_grad = jnp.einsum(
        "qhd,khd->hqk", attended_grad, values_part, preferred_element_type=jnp.float32
    )
    rowdot = jnp.sum(probabilities * weight_grad, axis=2, keepdims=True)
    score_grad = (probabilities * (weight_grad - rowdot)).astype(jnp.bfloat16)
    query_grad = (
        jnp.einsum("hqk,khd->qhd", score_grad, keys_part, preferred_element_type=jnp.float32)
        * scale_factor
    )
    key_grad = (
        jnp.einsum("hqk,qhd->khd", score_grad, queries, preferred_element_type=jnp.float32)
        * scale_factor
    )
    projected_grad = jnp.stack(
        [
            query_grad.reshape(rows_count, part_width),
            key_grad.reshape(rows_count, part_width),
            values_grad.reshape(rows_count, part_width),
        ],
        axis=1,
    ).astype(jnp.bfloat16)
    flat_grad = projected_grad.reshape(rows_count, 3 * part_width)
    qkv_grad = contract_rows(first_normalized, flat_grad).reshape(hidden_width, 3, part_width)
    qv_add_grad = jnp.stack(
        [
            jnp.sum(projected_grad[:, 0].astype(jnp.float32), axis=0),
            jnp.sum(projected_grad[:, 2].astype(jnp.float32), axis=0),
        ]
    )
    first_normalized_gradient = lax.psum_scatter(
        contract_cols(flat_grad, qkv_mat.reshape(hidden_width, 3 * part_width)),
        "tensor",
        scatter_dimension=1,
        tiled=True,
    )
    first_centered_unit = (
        partial_residual.astype(jnp.float32) - first_row_averages
    ) * first_inverse_deviation
    first_gain_gradient = jnp.sum(first_normalized_gradient * first_centered_unit, axis=0)
    bias_one_grad = jnp.sum(first_normalized_gradient, axis=0)
    first_rescaled = first_normalized_gradient * local_part(first_norm_gain)
    third_running_total, fourth_running_total = lax.psum(
        (
            jnp.sum(first_rescaled, axis=1, keepdims=True),
            jnp.sum(first_rescaled * first_centered_unit, axis=1, keepdims=True),
        ),
        "tensor",
    )
    stream_grad = middle_grad + first_inverse_deviation * (
        first_rescaled
        - third_running_total / hidden_width
        - first_centered_unit * fourth_running_total / hidden_width
    )
    attention_grads = (
        first_gain_gradient,
        bias_one_grad,
        qkv_grad,
        qv_add_grad,
        out_grad,
        out_add_grad,
    )
    attention_grads = tuple((older + newer for older, newer in zip(grad_sums[:6], attention_grads)))
    return (stream_grad, attention_grads + feed_grads)


def shards(
    images,
    slot_table,
    ln1_gain,
    ln1_bias,
    qkv_weight,
    qv_bias,
    out_weight,
    out_bias,
    ln2_gain,
    ln2_bias,
    fc1_weight,
    fc1_bias,
    fc2_weight,
    fc2_bias,
    cotangent,
):
    params = tuple(
        (
            weight_arg[0]
            for weight_arg in (
                ln1_gain,
                ln1_bias,
                qkv_weight,
                qv_bias,
                out_weight,
                out_bias,
                ln2_gain,
                ln2_bias,
                fc1_weight,
                fc1_bias,
                fc2_weight,
                fc2_bias,
            )
        )
    )
    section_index = lax.axis_index("section")
    part_width = images.shape[2]
    column = lax.axis_index("tensor") * part_width
    slot_count = images.shape[0]
    micro_count = slot_table.shape[0]
    slot_ids = jnp.arange(slot_count, dtype=jnp.int32)

    def locate(batch_index):
        clipped = jnp.clip(batch_index, 0, micro_count - 1)
        chosen = lax.dynamic_index_in_dim(slot_table, clipped, 0, keepdims=False)
        active = (batch_index >= 0) & (batch_index < micro_count) & (chosen < slot_count)
        return (jnp.minimum(chosen, slot_count - 1), active, (slot_ids == chosen) & active)

    received = jnp.zeros(images.shape[1:], jnp.bfloat16)
    layer_outputs = jnp.zeros(images.shape, jnp.bfloat16)
    saved_states = []
    for step_index in range(micro_count + 1):
        where_from, active, placed = locate(step_index - section_index)
        own_image = lax.dynamic_index_in_dim(images, where_from, 0, keepdims=False)
        entering = jnp.where(section_index == 0, own_image, received)
        leaving, layer_state = layer_forward(entering, params, column)
        saved_states.append(layer_state)
        layer_outputs = layer_outputs + placed[:, None, None].astype(jnp.bfloat16) * leaving[None]
        if step_index < micro_count:
            received = shifted(leaving, "section", 1)

    def zeros_of(extent):
        return jnp.zeros(extent, jnp.float32)

    grad_sums = (
        zeros_of((part_width,)),
        zeros_of((part_width,)),
        zeros_of(params[2].shape),
        zeros_of(params[3].shape),
        zeros_of(params[4].shape),
        zeros_of((part_width,)),
        zeros_of((part_width,)),
        zeros_of((part_width,)),
        zeros_of(params[8].shape),
        zeros_of(params[9].shape),
        zeros_of(params[10].shape),
        zeros_of((part_width,)),
    )
    coming_back = jnp.zeros(images.shape[1:], jnp.bfloat16)
    grads_in = jnp.zeros(images.shape, jnp.float32)
    for step_index in range(micro_count + 1):
        where_from, active, placed = locate(micro_count - step_index - section_index)
        own_grad = lax.dynamic_index_in_dim(cotangent, where_from, 0, keepdims=False)
        entering = jnp.where(section_index == 1, own_grad, coming_back).astype(
            jnp.float32
        ) * active.astype(jnp.float32)
        stream_grad, grad_sums = layer_backward(
            entering, saved_states[micro_count - step_index], params, column, grad_sums
        )
        grads_in = grads_in + placed[:, None, None].astype(jnp.float32) * stream_grad[None]
        if step_index < micro_count:
            coming_back = shifted(stream_grad.astype(jnp.bfloat16), "section", -1)
    grad_sums = member_sum(grad_sums)
    return (layer_outputs[None], grads_in[None]) + tuple((gradient[None] for gradient in grad_sums))


def solution(mesh):
    in_specs = (
        P("dp", None, "tensor"),
        P("dp"),
        P("section", None),
        P("section", None),
        P("section", None, None, "tensor"),
        P("section", None, "tensor"),
        P("section", "tensor", None),
        P("section", None),
        P("section", None),
        P("section", None),
        P("section", None, "tensor"),
        P("section", "tensor"),
        P("section", "tensor", None),
        P("section", None),
        P("dp", None, "tensor"),
    )
    out_specs = (
        P("section", "dp", None, "tensor"),
        P("section", "dp", None, "tensor"),
        P("section", "tensor"),
        P("section", "tensor"),
        P("section", None, None, "tensor"),
        P("section", None, "tensor"),
        P("section", "tensor", None),
        P("section", "tensor"),
        P("section", "tensor"),
        P("section", "tensor"),
        P("section", None, "tensor"),
        P("section", "tensor"),
        P("section", "tensor", None),
        P("section", "tensor"),
    )
    return jax.shard_map(shards, mesh=mesh, in_specs=in_specs, out_specs=out_specs, check_vma=False)
```

profile of v0, /device:TPU:0, one launch (start us, length us, event | category | flops | bytes accessed | tf_op | source)
XLA Modules:
  0.0 948.4 jit_solution(2319730954363733079)
XLA Ops:
  10.3 12.1 %all-gather = bf16[1,577,768]{1,2,0:T(8,128)(2,1)S(1)} all-gather(bf16[1,577,192]{1,2,0:T(8,128)(2,1)S(1)} %dynamic-slice_select_fusion.1), channel_id=2, replica_groups=mesh['section'=2,'dp'=16,'tensor'=4] {'tensor'}, dimensions={2}, use_global_device_ids=true | all-gather | bytes 1107840 | tf_op jit(solution)/shard_map/all_gather | solution.py:66
  35.2 38.0 %reduce-scatter.13.cloned.1.call-done = f32[577,192]{0,1:T(8,128)} async-done(((f32[577,768]{0,1:T(8,128)}), f32[577,192]{0,1:T(8,128)}) %reduce-scatter.13.cloned.1.call-update) | async-done | bytes 443152 | tf_op jit(solution)/shard_map/reduce_scatter | solution.py:98
  74.3 11.1 %all_gather.37 = bf16[577,768]{0,1:T(8,128)(2,1)S(1)} all-gather(bf16[577,192]{0,1:T(8,128)(2,1)S(1)} %fusion.150), channel_id=1, replica_groups=mesh['section'=2,'dp'=16,'tensor'=4] {'tensor'}, dimensions={1}, use_global_device_ids=true | all-gather | bytes 1107840 | tf_op jit(solution)/shard_map/all_gather | solution.py:105
  96.7 36.3 %reduce-scatter.15.cloned.1.call-done = f32[577,192]{0,1:T(8,128)} async-done(((f32[577,768]{0,1:T(8,128)}), f32[577,192]{0,1:T(8,128)}) %reduce-scatter.15.cloned.1.call-update) | async-done | bytes 443152 | tf_op jit(solution)/shard_map/reduce_scatter | solution.py:116
  142.1 10.7 %all_gather.38 = bf16[577,768]{0,1:T(8,128)(2,1)S(1)} all-gather(bf16[577,192]{0,1:T(8,128)(2,1)S(1)} %bitcast_select_fusion.3), channel_id=1, replica_groups=mesh['section'=2,'dp'=16,'tensor'=4] {'tensor'}, dimensions={1}, use_global_device_ids=true | all-gather | bytes 1107840 | tf_op jit(solution)/shard_map/all_gather | solution.py:66
  160.6 40.3 %reduce-scatter.17.cloned.1.call-done = f32[577,192]{0,1:T(8,128)} async-done(((f32[577,768]{0,1:T(8,128)}), f32[577,192]{0,1:T(8,128)}) %reduce-scatter.17.cloned.1.call-update) | async-done | bytes 443152 | tf_op jit(solution)/shard_map/reduce_scatter | solution.py:98
  202.0 10.8 %all_gather.39 = bf16[577,768]{0,1:T(8,128)(2,1)S(1)} all-gather(bf16[577,192]{0,1:T(8,128)(2,1)S(1)} %fusion.152), channel_id=1, replica_groups=mesh['section'=2,'dp'=16,'tensor'=4] {'tensor'}, dimensions={1}, use_global_device_ids=true | all-gather | bytes 1107840 | tf_op jit(solution)/shard_map/all_gather | solution.py:105
  223.5 36.8 %reduce-scatter.19.cloned.1.call-done = f32[577,192]{0,1:T(8,128)} async-done(((f32[577,768]{0,1:T(8,128)}), f32[577,192]{0,1:T(8,128)}) %reduce-scatter.19.cloned.1.call-update) | async-done | bytes 443152 | tf_op jit(solution)/shard_map/reduce_scatter | solution.py:116
  272.2 10.2 %all_gather.40 = bf16[577,768]{0,1:T(8,128)(2,1)S(1)} all-gather(bf16[577,192]{0,1:T(8,128)(2,1)S(1)} %bitcast_select_fusion.2), channel_id=1, replica_groups=mesh['section'=2,'dp'=16,'tensor'=4] {'tensor'}, dimensions={1}, use_global_device_ids=true | all-gather | bytes 1107840 | tf_op jit(solution)/shard_map/all_gather | solution.py:66
  293.1 11.7 %all_gather.42 = bf16[577,768]{0,1:T(8,128)(2,1)} all-gather(bf16[577,192]{0,1:T(8,128)(2,1)S(1)} %get-tuple-element.97), channel_id=1, replica_groups=mesh['section'=2,'dp'=16,'tensor'=4] {'tensor'}, dimensions={1}, use_global_device_ids=true | all-gather | bytes 1107840 | tf_op jit(solution)/shard_map/all_gather | solution.py:183
  304.8 25.3 %reduce-scatter.21.cloned.1.call-done = f32[577,192]{0,1:T(8,128)} async-done(((f32[577,768]{0,1:T(8,128)}), f32[577,192]{0,1:T(8,128)}) %reduce-scatter.21.cloned.1.call-update) | async-done | bytes 443152 | tf_op jit(solution)/shard_map/reduce_scatter | solution.py:98
  331.3 10.8 %all_gather.41 = bf16[577,768]{0,1:T(8,128)(2,1)S(1)} all-gather(bf16[577,192]{0,1:T(8,128)(2,1)S(1)} %fusion.151), channel_id=1, replica_groups=mesh['section'=2,'dp'=16,'tensor'=4] {'tensor'}, dimensions={1}, use_global_device_ids=true | all-gather | bytes 1107840 | tf_op jit(solution)/shard_map/all_gather | solution.py:105
  354.6 36.3 %reduce-scatter.25.cloned.1.call-done = f32[577,192]{0,1:T(8,128)} async-done(((f32[577,768]{0,1:T(8,128)}), f32[577,192]{0,1:T(8,128)}) %reduce-scatter.25.cloned.1.call-update) | async-done | bytes 443152 | tf_op jit(solution)/shard_map/reduce_scatter | solution.py:191
  404.3 11.9 %all_gather.43 = bf16[577,768]{0,1:T(8,128)(2,1)S(1)} all-gather(bf16[577,192]{0,1:T(8,128)(2,1)S(1)} %convert_element_type.415), channel_id=1, replica_groups=mesh['section'=2,'dp'=16,'tensor'=4] {'tensor'}, dimensions={1}, use_global_device_ids=true | all-gather | bytes 1107840 | tf_op jit(solution)/shard_map/all_gather | solution.py:222
  433.5 32.3 %reduce-scatter.27.cloned.1.call-done = f32[577,192]{0,1:T(8,128)} async-done(((f32[577,768]{0,1:T(8,128)}), f32[577,192]{0,1:T(8,128)}) %reduce-scatter.27.cloned.1.call-update) | async-done | bytes 443152 | tf_op jit(solution)/shard_map/reduce_scatter | solution.py:269
  477.0 29.1 %reduce-scatter.23.cloned.1.call-done = f32[577,192]{0,1:T(8,128)} async-done(((f32[577,768]{0,1:T(8,128)}), f32[577,192]{0,1:T(8,128)}) %reduce-scatter.23.cloned.1.call-update) | async-done | bytes 443152 | tf_op jit(solution)/shard_map/reduce_scatter | solution.py:116
  539.2 37.8 %reduce-scatter.29.cloned.1.call-done = f32[577,192]{0,1:T(8,128)} async-done(((f32[577,768]{0,1:T(8,128)}), f32[577,192]{0,1:T(8,128)}) %reduce-scatter.29.cloned.1.call-update) | async-done | bytes 443152 | tf_op jit(solution)/shard_map/reduce_scatter | solution.py:191
  588.2 11.7 %all_gather.45 = bf16[577,768]{0,1:T(8,128)(2,1)S(1)} all-gather(bf16[577,192]{0,1:T(8,128)(2,1)S(1)} %convert_element_type.427), channel_id=1, replica_groups=mesh['section'=2,'dp'=16,'tensor'=4] {'tensor'}, dimensions={1}, use_global_device_ids=true | all-gather | bytes 1107840 | tf_op jit(solution)/shard_map/all_gather | solution.py:222
  612.4 37.0 %reduce-scatter.31.cloned.1.call-done = f32[577,192]{0,1:T(8,128)} async-done(((f32[577,768]{0,1:T(8,128)}), f32[577,192]{0,1:T(8,128)}) %reduce-scatter.31.cloned.1.call-update) | async-done | bytes 443152 | tf_op jit(solution)/shard_map/reduce_scatter | solution.py:269
  694.3 33.6 %reduce-scatter.33.cloned.1.call-done = f32[577,192]{0,1:T(8,128)} async-done(((f32[577,768]{0,1:T(8,128)}), f32[577,192]{0,1:T(8,128)}) %reduce-scatter.33.cloned.1.call-update) | async-done | bytes 443152 | tf_op jit(solution)/shard_map/reduce_scatter | solution.py:191
  738.7 11.5 %all_gather.47 = bf16[577,768]{0,1:T(8,128)(2,1)S(1)} all-gather(bf16[577,192]{0,1:T(8,128)(2,1)S(1)} %convert_element_type.439), channel_id=1, replica_groups=mesh['section'=2,'dp'=16,'tensor'=4] {'tensor'}, dimensions={1}, use_global_device_ids=true | all-gather | bytes 1107840 | tf_op jit(solution)/shard_map/all_gather | solution.py:222
  788.6 11.1 %reduce-scatter.35.cloned.1.call-done = f32[577,192]{0,1:T(8,128)} async-done(((f32[577,768]{0,1:T(8,128)}), f32[577,192]{0,1:T(8,128)}) %reduce-scatter.35.cloned.1.call-update) | async-done | bytes 443152 | tf_op jit(solution)/shard_map/reduce_scatter | solution.py:269
  801.1 75.7 %all-reduce = (f32[1,192]{1,0:T(1,128)}, f32[1,192]{1,0:T(1,128)}, f32[1,2,192]{2,1,0:T(2,128)}, f32[1,192]{1,0:T(1,128)}, f32[1,192]{1,0:T(1,128)}, /*index=5*/...) all-reduce(f32[1,192]{1,0:T(1,128)S(1)} %bitcast.365, ...), channel_id=1, replica_groups=mesh['section'=2,'dp'=16,'tensor'=4] {'dp'}, use_global_device_ids=true, to_apply=%region_60.61 | all-reduce | flops 2304 | bytes 18432 | tf_op jit(solution)/shard_map/psum | solution.py:40
  888.1 45.8 %all-reduce.10.cloned.1.call-done = (f32[1,768,3,192]{1,3,2,0:T(8,128)}, f32[1,192,768]{2,1,0:T(8,128)}, f32[1,768,768]{2,1,0:T(8,128)}, f32[1,768,768]{2,1,0:T(8,128)}) async-done(((f32[1,768,3,192]{1,3,2,0:T(8,128)}, f32[1,192,768]{2,1,0:T(8,128)}, f32[1,768,768]{2,1,0:T(8,128)}, f32[1,768,768]{2,1,0:T(8,128)}), (f32[1,768,3,192]{1,3,2,0:T(8,128)}, f32[1,192,768]{2,1,0:T(8,128)}, ...) | async-done | bytes 7077904 | tf_op jit(solution)/shard_map/psum | solution.py:40
  (504 shorter events, 300.8 us)
Async XLA Ops:
  7.2 78.7 %copy-start = (bf16[1,768,768]{2,1,0:T(8,128)(2,1)S(1)}, bf16[1,768,768]{2,1,0:T(8,128)(2,1)}, u32[]{:S(2)}) copy-start(bf16[1,768,768]{2,1,0:T(8,128)(2,1)} %param.25) | copy-start | bytes 3538948
  7.2 66.0 %reduce-scatter.13.cloned.1.call-start = ((), (), s32[]{:S(2)}) async-start(), calls=%async_computation.12 | async-start | bytes 2457600 | tf_op jit(solution)/shard_map/reduce_scatter | solution.py:98
  23.0 259.9 %copy-start.101 = (f32[768]{0:T(1024)}, f32[768]{0:T(1024)S(1)}, u32[]{:S(2)}) copy-start(f32[768]{0:T(1024)S(1)} %reduce.8) | copy-start | bytes 9220
  23.0 130.4 %copy-start.103 = (f32[768]{0:T(1024)}, f32[768]{0:T(1024)S(1)}, u32[]{:S(2)}) copy-start(f32[768]{0:T(1024)S(1)} %reduce.9) | copy-start | bytes 9220
  34.2 98.7 %reduce-scatter.15.cloned.1.call-start = ((), (), s32[]{:S(2)}) async-start(), calls=%async_computation.13 | async-start | bytes 2457600 | tf_op jit(solution)/shard_map/reduce_scatter | solution.py:116
  34.4 178.9 %copy-start.106 = (f32[768]{0:T(1024)}, f32[768]{0:T(1024)S(1)}, u32[]{:S(2)}) copy-start(f32[768]{0:T(1024)S(1)} %reduce.14) | copy-start | bytes 9220
  95.9 104.9 %reduce-scatter.17.cloned.1.call-start = ((), (), s32[]{:S(2)}) async-start(), calls=%async_computation.14 | async-start | bytes 2457600 | tf_op jit(solution)/shard_map/reduce_scatter | solution.py:98
  134.3 7.8 collective-permute-start
  142.1 58.7 %copy-start.6 = (bf16[577,192]{0,1:T(8,128)(2,1)}, bf16[577,192]{0,1:T(8,128)(2,1)S(1)}, u32[]{:S(2)}) copy-start(bf16[577,192]{0,1:T(8,128)(2,1)S(1)} %bitcast_select_fusion.3) | copy-start | bytes 664708
  160.5 99.8 %reduce-scatter.19.cloned.1.call-start = ((), (), s32[]{:S(2)}) async-start(), calls=%async_computation.15 | async-start | bytes 2457600 | tf_op jit(solution)/shard_map/reduce_scatter | solution.py:116
  223.3 106.8 %reduce-scatter.21.cloned.1.call-start = ((), (), s32[]{:S(2)}) async-start(), calls=%async_computation.16 | async-start | bytes 2457600 | tf_op jit(solution)/shard_map/reduce_scatter | solution.py:98
  262.5 8.1 collective-permute-start.1
  290.7 100.1 %reduce-scatter.25.cloned.1.call-start = ((), (), s32[]{:S(2)}) async-start(), calls=%async_computation.18 | async-start | bytes 2457600 | tf_op jit(solution)/shard_map/reduce_scatter | solution.py:191
  353.8 112.0 %reduce-scatter.27.cloned.1.call-start = ((), (), s32[]{:S(2)}) async-start(), calls=%async_computation.19 | async-start | bytes 2457600 | tf_op jit(solution)/shard_map/reduce_scatter | solution.py:269
  428.6 77.5 %reduce-scatter.23.cloned.1.call-start = ((), (), s32[]{:S(2)}) async-start(), calls=%async_computation.17 | async-start | bytes 2457600 | tf_op jit(solution)/shard_map/reduce_scatter | solution.py:116
  432.6 144.3 %reduce-scatter.29.cloned.1.call-start = ((), (), s32[]{:S(2)}) async-start(), calls=%async_computation.20 | async-start | bytes 2457600 | tf_op jit(solution)/shard_map/reduce_scatter | solution.py:191
  508.9 10.0 %collective-permute-start.2 = (bf16[577,192]{0,1:T(8,128)(2,1)}, bf16[577,192]{0,1:T(8,128)(2,1)}, u32[]{:S(2)}, u32[]{:S(2)}) collective-permute-start(bf16[577,192]{0,1:T(8,128)(2,1)} %get-tuple-element.82), channel_id=1, source_target_pairs={{64,0},{65,1},{66,2},{67,3},{68,4},{69,5},{70,6},{71,7},{72,8},{73... | collective-permute-start | bytes 664712 | tf_op jit(solution)/shard_map/ppermute | solution.py:17
  539.1 110.3 %reduce-scatter.31.cloned.1.call-start = ((), (), s32[]{:S(2)}) async-start(), calls=%async_computation.21 | async-start | bytes 2457600 | tf_op jit(solution)/shard_map/reduce_scatter | solution.py:269
  612.4 115.5 %reduce-scatter.33.cloned.1.call-start = ((), (), s32[]{:S(2)}) async-start(), calls=%async_computation.22 | async-start | bytes 2457600 | tf_op jit(solution)/shard_map/reduce_scatter | solution.py:191
  661.1 9.9 %collective-permute-start.3 = (bf16[577,192]{0,1:T(8,128)(2,1)}, bf16[577,192]{0,1:T(8,128)(2,1)}, u32[]{:S(2)}, u32[]{:S(2)}) collective-permute-start(bf16[577,192]{0,1:T(8,128)(2,1)} %get-tuple-element.80), channel_id=1, source_target_pairs={{64,0},{65,1},{66,2},{67,3},{68,4},{69,5},{70,6},{71,7},{72,8},{73... | collective-permute-start | bytes 664712 | tf_op jit(solution)/shard_map/ppermute | solution.py:17
  690.2 109.5 %reduce-scatter.35.cloned.1.call-start = ((), (), s32[]{:S(2)}) async-start(), calls=%async_computation.23 | async-start | bytes 2457600 | tf_op jit(solution)/shard_map/reduce_scatter | solution.py:269
  762.6 171.3 %all-reduce.10.cloned.1.call-start = ((), (), s32[]{:S(2)}) async-start(), calls=%async_computation.24 | async-start | bytes 14155776 | tf_op jit(solution)/shard_map/psum | solution.py:40
  785.8 98.6 %copy-start.31 = (f32[577,192]{0,1:T(8,128)S(1)}, f32[577,192]{0,1:T(8,128)}, u32[]{:S(2)}) copy-start(f32[577,192]{0,1:T(8,128)} %copy-done.30) | copy-start | bytes 1329412
  788.1 97.6 %copy-start.63 = (f32[577,192]{0,1:T(8,128)S(1)}, f32[577,192]{0,1:T(8,128)}, u32[]{:S(2)}) copy-start(f32[577,192]{0,1:T(8,128)} %get-tuple-element.83) | copy-start | bytes 1329412
  (137 other events, 630.8 us)
Sparse Core Ops, SparseCore 0:
  34.3 38.7 reduce-scatter.12
  96.0 36.9 reduce-scatter.14
  160.6 40.1 reduce-scatter.16
  223.4 36.9 reduce-scatter.18
  290.8 39.2 reduce-scatter.20
  353.9 36.9 reduce-scatter.24
  428.7 36.9 reduce-scatter.26
  469.2 36.8 reduce-scatter.22
  539.2 37.6 reduce-scatter.28
  612.5 36.9 reduce-scatter.30
  690.3 37.5 reduce-scatter.32
  762.7 36.9 reduce-scatter.34
  804.6 129.2 all-reduce.9
where the time goes:
time: 955 us; the launch traced here: 948 us
  waiting for transfers between devices  464 us (49%)
  blocking collectives  254 us (27%)
  matrix products  110 us (12%)
  other arithmetic  54.9 us (6%)
  local copies, waits for them, and re-layouts  36.6 us (4%)
  between operations  19.8 us (2%)
  starting transfers between devices  10.1 us (1%)
    reduce_scatter x3, waiting for transfers between devices, layer_backward(): lax.psum_scatter(contract_cols(pre_grad, up_mat), 'tensor', scatter_dimen...  108 us
    reduce_scatter x3, waiting for transfers between devices, layer_forward(): lax.psum_scatter(jnp.dot(attended, out_mat, preferred_element_type=jnp.fl...  104 us
    reduce_scatter x3, waiting for transfers between devices, layer_forward(): lax.psum_scatter(jnp.dot(hidden, down_mat, preferred_element_type=jnp.flo...  102 us
    reduce_scatter x3, waiting for transfers between devices, layer_backward(): lax.psum_scatter(contract_cols(flat_grad, qkv_mat.reshape(hidden_width, 3...  80.4 us
    psum x1, blocking collectives, member_sum(): return lax.psum(gradients, 'dp')  75.7 us
    psum x1, waiting for transfers between devices, member_sum(): return lax.psum(gradients, 'dp')  45.8 us
    all_gather x3, blocking collectives, layer_backward(): lax.all_gather(middle_grad.astype(jnp.bfloat16), 'tensor', axis=1, tiled=...  35.1 us
    all_gather x3, blocking collectives, layer_forward(): lax.all_gather(partial_residual, 'tensor', axis=1, tiled=True)  33 us
  transfers between devices with their start and end apart: 17, of which 17 were waited for; matrix products, arithmetic and copies ran while one was open for 5% of the time, Pallas kernels for 0%

commit v1 on v0

--- a/solution.py
+++ b/solution.py
@@ -38,6 +38,10 @@
 
 def member_sum(gradients):
     return lax.psum(gradients, "dp")
+
+
+def tensor_sum(partial_value):
+    return lax.psum(partial_value.astype(jnp.bfloat16), "tensor").astype(jnp.float32)
 
 
 def layer_forward(partial_residual, params, column):
@@ -60,12 +64,11 @@
     hidden_width = first_norm_gain.shape[0]
     head_count = part_width // HD
 
-    def local_part(vector):
-        return lax.dynamic_slice_in_dim(vector, column, part_width, 0)
-
-    complete_residual = lax.all_gather(partial_residual, "tensor", axis=1, tiled=True)
+    complete_residual = lax.all_gather(partial_residual, "tensor", axis=1, tiled=True).astype(
+        jnp.float32
+    )
     first_centered_unit, first_row_averages, first_inverse_deviation = standardize_rows(
-        complete_residual.astype(jnp.float32)
+        complete_residual
     )
     first_normalized = (first_centered_unit * first_norm_gain + first_norm_bias).astype(
         jnp.bfloat16
@@ -95,34 +98,22 @@
         .reshape(rows_count, part_width)
         .astype(jnp.bfloat16)
     )
-    branch = lax.psum_scatter(
-        jnp.dot(attended, out_mat, preferred_element_type=jnp.float32),
-        "tensor",
-        scatter_dimension=1,
-        tiled=True,
-    )
-    middle = partial_residual.astype(jnp.float32) + branch + local_part(out_add)
-    complete_middle_state = lax.all_gather(
-        middle.astype(jnp.bfloat16), "tensor", axis=1, tiled=True
-    )
+    branch = tensor_sum(jnp.dot(attended, out_mat, preferred_element_type=jnp.float32))
+    middle = complete_residual + branch + out_add
+    middle_rounded = middle.astype(jnp.bfloat16).astype(jnp.float32)
     second_centered_unit, second_row_averages, second_inverse_deviation = standardize_rows(
-        complete_middle_state.astype(jnp.float32)
+        middle_rounded
     )
     second_normalized = (second_centered_unit * second_norm_gain + second_norm_bias).astype(
         jnp.bfloat16
     )
     hidden_pre = jnp.dot(second_normalized, up_mat, preferred_element_type=jnp.float32) + up_add
     hidden = jax.nn.gelu(hidden_pre, approximate=False).astype(jnp.bfloat16)
-    feed_out = lax.psum_scatter(
-        jnp.dot(hidden, down_mat, preferred_element_type=jnp.float32),
-        "tensor",
-        scatter_dimension=1,
-        tiled=True,
-    )
-    result = middle + feed_out + local_part(down_add)
+    feed_out = tensor_sum(jnp.dot(hidden, down_mat, preferred_element_type=jnp.float32))
+    result = middle + feed_out + down_add
+    result_part = lax.dynamic_slice_in_dim(result, column, part_width, 1)
     saved_state = (
-        partial_residual,
-        first_row_averages,
+        first_centered_unit,
         first_inverse_deviation,
         first_normalized,
         queries,
@@ -130,14 +121,13 @@
         values_part,
         totals,
         attended,
-        complete_middle_state,
-        second_row_averages,
+        second_centered_unit,
         second_inverse_deviation,
         second_normalized,
         hidden_pre,
         hidden,
     )
-    return (result.astype(jnp.bfloat16), saved_state)
+    return (result_part.astype(jnp.bfloat16), saved_state)
 
 
 def layer_backward(grad_part, saved_state, params, column, grad_sums):
@@ -156,8 +146,7 @@
         down_add,
     ) = params
     (
-        partial_residual,
-        first_row_averages,
+        first_centered_unit,
         first_inverse_deviation,
         first_normalized,
         queries,
@@ -165,8 +154,7 @@
         values_part,
         totals,
         attended,
-        complete_middle_state,
-        second_row_averages,
+        second_centered_unit,
         second_inverse_deviation,
         second_normalized,
         hidden_pre,
@@ -177,35 +165,25 @@
     hidden_width = first_norm_gain.shape[0]
     head_count = part_width // HD
 
-    def local_part(vector):
-        return lax.dynamic_slice_in_dim(vector, column, part_width, 0)
-
-    grad_full = lax.all_gather(grad_part.astype(jnp.bfloat16), "tensor", axis=1, tiled=True)
-    down_grad = contract_rows(hidden, grad_full)
-    down_add_grad = jnp.sum(grad_part, axis=0)
-    hidden_grad = contract_cols(grad_full, down_mat)
+    def local_cols(matrix):
+        return lax.dynamic_slice_in_dim(matrix, column, part_width, 1)
+
+    grad_full_bf16 = lax.all_gather(grad_part, "tensor", axis=1, tiled=True)
+    grad_full = grad_full_bf16.astype(jnp.float32)
+    down_grad = contract_rows(hidden, grad_full_bf16)
+    down_add_grad = jnp.sum(local_cols(grad_full), axis=0)
+    hidden_grad = contract_cols(grad_full_bf16, down_mat)
     unused_value, gelu_back = jax.vjp(partial(jax.nn.gelu, approximate=False), hidden_pre)
     pre_grad = gelu_back(hidden_grad)[0].astype(jnp.bfloat16)
     up_grad = contract_rows(second_normalized, pre_grad)
     up_add_grad = jnp.sum(pre_grad.astype(jnp.float32), axis=0)
-    normalized_gradient = lax.psum_scatter(
-        contract_cols(pre_grad, up_mat), "tensor", scatter_dimension=1, tiled=True
-    )
-    local_middle_state = lax.dynamic_slice_in_dim(
-        complete_middle_state, column, part_width, 1
-    ).astype(jnp.float32)
-    second_centered_unit = (local_middle_state - second_row_averages) * second_inverse_deviation
-    second_gain_gradient = jnp.sum(normalized_gradient * second_centered_unit, axis=0)
-    bias_two_grad = jnp.sum(normalized_gradient, axis=0)
-    second_rescaled = normalized_gradient * local_part(second_norm_gain)
-    first_running_total, second_running_total = lax.psum(
-        (
-            jnp.sum(second_rescaled, axis=1, keepdims=True),
-            jnp.sum(second_rescaled * second_centered_unit, axis=1, keepdims=True),
-        ),
-        "tensor",
-    )
-    middle_grad = grad_part + second_inverse_deviation * (
+    normalized_gradient = tensor_sum(contract_cols(pre_grad, up_mat))
+    second_gain_gradient = jnp.sum(local_cols(normalized_gradient * second_centered_unit), axis=0)
+    bias_two_grad = jnp.sum(local_cols(normalized_gradient), axis=0)
+    second_rescaled = normalized_gradient * second_norm_gain
+    first_running_total = jnp.sum(second_rescaled, axis=1, keepdims=True)
+    second_running_total = jnp.sum(second_rescaled * second_centered_unit, axis=1, keepdims=True)
+    middle_grad = grad_full + second_inverse_deviation * (
         second_rescaled
         - first_running_total / hidden_width
         - second_centered_unit * second_running_total / hidden_width
@@ -219,9 +197,9 @@
         down_add_grad,
     )
     feed_grads = tuple((older + newer for older, newer in zip(grad_sums[6:], feed_grads)))
-    branch_grad = lax.all_gather(middle_grad.astype(jnp.bfloat16), "tensor", axis=1, tiled=True)
+    branch_grad = middle_grad.astype(jnp.bfloat16)
     out_grad = contract_rows(attended, branch_grad)
-    out_add_grad = jnp.sum(middle_grad, axis=0)
+    out_add_grad = jnp.sum(local_cols(middle_grad), axis=0)
     attended_grad = (
         contract_cols(branch_grad, out_mat).astype(jnp.bfloat16).reshape(rows_count, head_count, HD)
     )
@@ -266,25 +244,16 @@
             jnp.sum(projected_grad[:, 2].astype(jnp.float32), axis=0),
         ]
     )
-    first_normalized_gradient = lax.psum_scatter(
-        contract_cols(flat_grad, qkv_mat.reshape(hidden_width, 3 * part_width)),
-        "tensor",
-        scatter_dimension=1,
-        tiled=True,
-    )
-    first_centered_unit = (
-        partial_residual.astype(jnp.float32) - first_row_averages
-    ) * first_inverse_deviation
-    first_gain_gradient = jnp.sum(first_normalized_gradient * first_centered_unit, axis=0)
-    bias_one_grad = jnp.sum(first_normalized_gradient, axis=0)
-    first_rescaled = first_normalized_gradient * local_part(first_norm_gain)
-    third_running_total, fourth_running_total = lax.psum(
-        (
-            jnp.sum(first_rescaled, axis=1, keepdims=True),
-            jnp.sum(first_rescaled * first_centered_unit, axis=1, keepdims=True),
-        ),
-        "tensor",
-    )
+    first_normalized_gradient = tensor_sum(
+        contract_cols(flat_grad, qkv_mat.reshape(hidden_width, 3 * part_width))
+    )
+    first_gain_gradient = jnp.sum(
+        local_cols(first_normalized_gradient * first_centered_unit), axis=0
+    )
+    bias_one_grad = jnp.sum(local_cols(first_normalized_gradient), axis=0)
+    first_rescaled = first_normalized_gradient * first_norm_gain
+    third_running_total = jnp.sum(first_rescaled, axis=1, keepdims=True)
+    fourth_running_total = jnp.sum(first_rescaled * first_centered_unit, axis=1, keepdims=True)
     stream_grad = middle_grad + first_inverse_deviation * (
         first_rescaled
         - third_running_total / hidden_width
@@ -299,7 +268,7 @@
         out_add_grad,
     )
     attention_grads = tuple((older + newer for older, newer in zip(grad_sums[:6], attention_grads)))
-    return (stream_grad, attention_grads + feed_grads)
+    return (local_cols(stream_grad), attention_grads + feed_grads)
 
 
 def shards(
@@ -386,9 +355,9 @@
     for step_index in range(micro_count + 1):
         where_from, active, placed = locate(micro_count - step_index - section_index)
         own_grad = lax.dynamic_index_in_dim(cotangent, where_from, 0, keepdims=False)
-        entering = jnp.where(section_index == 1, own_grad, coming_back).astype(
-            jnp.float32
-        ) * active.astype(jnp.float32)
+        entering = jnp.where(
+            active, jnp.where(section_index == 1, own_grad, coming_back), jnp.zeros_like(own_grad)
+        )
         stream_grad, grad_sums = layer_backward(
             entering, saved_states[micro_count - step_index], params, column, grad_sums
         )

time: 955 us -> 913 us (0.956)
  blocking collectives: 254 us -> 142 us
  waiting for transfers between devices: 464 us -> 522 us
  other arithmetic: 54.9 us -> 69.1 us
    psum x0 -> x11, waiting for transfers between devices: none -> 447 us  [tensor_sum(): lax.psum(partial_value.astype(jnp.bfloat16), 'tensor').astype(jnp.float32)]
    reduce_scatter x12 -> x0, waiting for transfers between devices: 394 us -> none  [the longest x3 108 us: layer_backward(): lax.psum_scatter(contract_cols(pre_grad, up_mat), 'tensor', scatter_dimen...]
    all_gather x9 -> x3, blocking collectives: 99.3 us -> 32.7 us  [layer_backward(): grad_full_bf16 = lax.all_gather(grad_part, 'tensor', axis=1, tiled=True)]
    psum x6 -> x0, blocking collectives: 45.7 us -> none  [the longest x3 23 us: layer_backward(): lax.psum((jnp.sum(first_rescaled, axis=1, keepdims=True), jnp.sum(first_r...]
    unnamed x292 -> x288, local copies, waits for them, and re-layouts: 30.4 us -> 32.2 us
  transfers between devices with their start and end apart: 17 -> 16, of which waited for: 17 -> 16; matrix products, arithmetic and copies ran while one was open for 5% -> 6% of each run, Pallas kernels for 0% -> 0%
where the time goes in v1:
time: 913 us; the launch traced here: 907 us
  waiting for transfers between devices  522 us (57%)
  blocking collectives  142 us (16%)
  matrix products  109 us (12%)
  other arithmetic  69.1 us (8%)
  local copies, waits for them, and re-layouts  34.1 us (4%)
  between operations  20.2 us (2%)
  starting transfers between devices  10.4 us (1%)
    psum x11, waiting for transfers between devices, tensor_sum(): lax.psum(partial_value.astype(jnp.bfloat16), 'tensor').astype(jnp.float32)  447 us
    psum x1, blocking collectives, member_sum(): return lax.psum(gradients, 'dp')  75.8 us
    psum x1, waiting for transfers between devices, member_sum(): return lax.psum(gradients, 'dp')  49.7 us
    all_gather x3, blocking collectives, layer_forward(): lax.all_gather(partial_residual, 'tensor', axis=1, tiled=True)  33.6 us
    all_gather x3, blocking collectives, layer_backward(): grad_full_bf16 = lax.all_gather(grad_part, 'tensor', axis=1, tiled=True)  32.7 us
    unnamed x288, local copies, waits for them, and re-layouts  32.2 us
    dot_general x12, matrix products, contract_rows(): lax.dot_general(left_side, right_side, (((0,), (0,)), ((), ())), preferre...  29.4 us
    ppermute x4, waiting for transfers between devices, shifted(): return lax.ppermute(block, axis, route)  24.3 us
  transfers between devices with their start and end apart: 16, of which 16 were waited for; matrix products, arithmetic and copies ran while one was open for 6% of the time, Pallas kernels for 0%

profile of v1, /device:TPU:0, one launch (start us, length us, event | category | flops | bytes accessed | tf_op | source)
XLA Modules:
  0.0 906.6 jit_solution(10177425742683341397)
XLA Ops:
  11.8 12.1 %all-gather = bf16[1,577,768]{1,2,0:T(8,128)(2,1)S(1)} all-gather(bf16[1,577,192]{1,2,0:T(8,128)(2,1)S(1)} %dynamic-slice_select_fusion), channel_id=2, replica_groups=mesh['section'=2,'dp'=16,'tensor'=4] {'tensor'}, dimensions={2}, use_global_device_ids=true | all-gather | bytes 1107840 | tf_op jit(solution)/shard_map/all_gather | solution.py:67
  32.4 45.7 %all-reduce.16.cloned.1.call-done = bf16[577,768]{0,1:T(8,128)(2,1)} async-done(((bf16[577,768]{0,1:T(8,128)(2,1)}), bf16[577,768]{0,1:T(8,128)(2,1)}) %all-reduce.16.cloned.1.call-update) | async-done | bytes 886288 | tf_op jit(solution)/shard_map/psum | solution.py:44
  81.3 6.5 multiply_convert_fusion.5
  91.1 44.4 %all-reduce.18.cloned.1.call-done = bf16[577,768]{0,1:T(8,128)(2,1)} async-done(((bf16[577,768]{0,1:T(8,128)(2,1)}), bf16[577,768]{0,1:T(8,128)(2,1)}) %all-reduce.18.cloned.1.call-update) | async-done | bytes 886288 | tf_op jit(solution)/shard_map/psum | solution.py:44
  145.9 11.0 %all_gather.19 = bf16[577,768]{0,1:T(8,128)(2,1)S(1)} all-gather(bf16[577,192]{0,1:T(8,128)(2,1)S(1)} %bitcast_select_fusion.3), channel_id=1, replica_groups=mesh['section'=2,'dp'=16,'tensor'=4] {'tensor'}, dimensions={1}, use_global_device_ids=true | all-gather | bytes 1107840 | tf_op jit(solution)/shard_map/all_gather | solution.py:67
  164.9 46.0 %all-reduce.20.cloned.1.call-done = bf16[577,768]{0,1:T(8,128)(2,1)} async-done(((bf16[577,768]{0,1:T(8,128)(2,1)}), bf16[577,768]{0,1:T(8,128)(2,1)}) %all-reduce.20.cloned.1.call-update) | async-done | bytes 886288 | tf_op jit(solution)/shard_map/psum | solution.py:44
  214.1 6.6 multiply_convert_fusion.4
  223.8 44.5 %all-reduce.22.cloned.1.call-done = bf16[577,768]{0,1:T(8,128)(2,1)} async-done(((bf16[577,768]{0,1:T(8,128)(2,1)}), bf16[577,768]{0,1:T(8,128)(2,1)}) %all-reduce.22.cloned.1.call-update) | async-done | bytes 886288 | tf_op jit(solution)/shard_map/psum | solution.py:44
  279.8 10.5 %all_gather.20 = bf16[577,768]{0,1:T(8,128)(2,1)S(1)} all-gather(bf16[577,192]{0,1:T(8,128)(2,1)S(1)} %bitcast_select_fusion.2), channel_id=1, replica_groups=mesh['section'=2,'dp'=16,'tensor'=4] {'tensor'}, dimensions={1}, use_global_device_ids=true | all-gather | bytes 1107840 | tf_op jit(solution)/shard_map/all_gather | solution.py:67
  300.0 11.7 %all-gather.1 = bf16[1,577,768]{1,2,0:T(8,128)(2,1)} all-gather(bf16[1,577,192]{1,2,0:T(8,128)(2,1)S(1)} %select_select_fusion), channel_id=3, replica_groups=mesh['section'=2,'dp'=16,'tensor'=4] {'tensor'}, dimensions={2}, use_global_device_ids=true | all-gather | bytes 1107840 | tf_op jit(solution)/shard_map/all_gather | solution.py:171
  311.7 33.5 %all-reduce.24.cloned.1.call-done = bf16[577,768]{0,1:T(8,128)(2,1)} async-done(((bf16[577,768]{0,1:T(8,128)(2,1)}), bf16[577,768]{0,1:T(8,128)(2,1)}) %all-reduce.24.cloned.1.call-update) | async-done | bytes 886288 | tf_op jit(solution)/shard_map/psum | solution.py:44
  348.7 5.8 multiply_convert_fusion.3
  359.9 44.4 %all-reduce.26.cloned.1.call-done = bf16[577,768]{0,1:T(8,128)(2,1)} async-done(((bf16[577,768]{0,1:T(8,128)(2,1)}), bf16[577,768]{0,1:T(8,128)(2,1)}) %all-reduce.26.cloned.1.call-update) | async-done | bytes 886288 | tf_op jit(solution)/shard_map/psum | solution.py:44
  422.3 44.6 %all-reduce.28.cloned.1.call-done = bf16[577,768]{0,1:T(8,128)(2,1)} async-done(((bf16[577,768]{0,1:T(8,128)(2,1)}), bf16[577,768]{0,1:T(8,128)(2,1)}) %all-reduce.28.cloned.1.call-update) | async-done | bytes 886288 | tf_op jit(solution)/shard_map/psum | solution.py:44
  473.3 8.5 collective-permute-done.2
  482.8 10.5 %all_gather.22 = bf16[577,768]{0,1:T(8,128)(2,1)S(1)} all-gather(bf16[577,192]{0,1:T(8,128)(2,1)S(1)} %fusion.133), channel_id=1, replica_groups=mesh['section'=2,'dp'=16,'tensor'=4] {'tensor'}, dimensions={1}, use_global_device_ids=true | all-gather | bytes 1107840 | tf_op jit(solution)/shard_map/all_gather | solution.py:171
  506.0 39.2 %all-reduce.30.cloned.1.call-done = bf16[577,768]{0,1:T(8,128)(2,1)} async-done(((bf16[577,768]{0,1:T(8,128)(2,1)}), bf16[577,768]{0,1:T(8,128)(2,1)}) %all-reduce.30.cloned.1.call-update) | async-done | bytes 886288 | tf_op jit(solution)/shard_map/psum | solution.py:44
  571.8 36.8 %all-reduce.32.cloned.1.call-done = bf16[577,768]{0,1:T(8,128)(2,1)} async-done(((bf16[577,768]{0,1:T(8,128)(2,1)}), bf16[577,768]{0,1:T(8,128)(2,1)}) %all-reduce.32.cloned.1.call-update) | async-done | bytes 886288 | tf_op jit(solution)/shard_map/psum | solution.py:44
  616.6 6.3 collective-permute-done.3
  623.9 10.5 %all_gather.23 = bf16[577,768]{0,1:T(8,128)(2,1)S(1)} all-gather(bf16[577,192]{0,1:T(8,128)(2,1)S(1)} %fusion.132), channel_id=1, replica_groups=mesh['section'=2,'dp'=16,'tensor'=4] {'tensor'}, dimensions={1}, use_global_device_ids=true | all-gather | bytes 1107840 | tf_op jit(solution)/shard_map/all_gather | solution.py:171
  647.8 36.2 %all-reduce.34.cloned.1.call-done = bf16[577,768]{0,1:T(8,128)(2,1)} async-done(((bf16[577,768]{0,1:T(8,128)(2,1)}), bf16[577,768]{0,1:T(8,128)(2,1)}) %all-reduce.34.cloned.1.call-update) | async-done | bytes 886288 | tf_op jit(solution)/shard_map/psum | solution.py:44
  725.5 32.2 %all-reduce.38.cloned.1.call-done = (bf16[577,768]{0,1:T(8,128)(2,1)}, bf16[577,768]{0,1:T(8,128)(2,1)}) async-done(((bf16[577,768]{0,1:T(8,128)(2,1)}, bf16[577,768]{0,1:T(8,128)(2,1)}), (bf16[577,768]{0,1:T(8,128)(2,1)}, bf16[577,768]{0,1:T(8,128)(2,1)})) %all-reduce.38.cloned.1.call-update) | async-done | bytes 1772560 | tf_op jit(solution)/shard_map/psum | solution.py:44
  761.6 75.8 %all-reduce = (f32[1,192]{1,0:T(1,128)}, f32[1,192]{1,0:T(1,128)}, f32[1,2,192]{2,1,0:T(2,128)}, f32[1,192]{1,0:T(1,128)}, f32[1,192]{1,0:T(1,128)}, /*index=5*/...) all-reduce(f32[1,192]{1,0:T(1,128)S(1)} %bitcast.331, ...), channel_id=1, replica_groups=mesh['section'=2,'dp'=16,'tensor'=4] {'dp'}, use_global_device_ids=true, to_apply=%region_48.49 | all-reduce | flops 2304 | bytes 18432 | tf_op jit(solution)/shard_map/psum | solution.py:40
  842.1 49.7 %all-reduce.36.cloned.1.call-done = (f32[1,768,3,192]{1,3,2,0:T(8,128)}, f32[1,192,768]{2,1,0:T(8,128)}, f32[1,768,768]{2,1,0:T(8,128)}, f32[1,768,768]{2,1,0:T(8,128)}) async-done(((f32[1,768,3,192]{1,3,2,0:T(8,128)}, f32[1,192,768]{2,1,0:T(8,128)}, f32[1,768,768]{2,1,0:T(8,128)}, f32[1,768,768]{2,1,0:T(8,128)}), (f32[1,768,3,192]{1,3,2,0:T(8,128)}, f32[1,192,768]{2,1,0:T(8,128)}, ...) | async-done | bytes 7077904 | tf_op jit(solution)/shard_map/psum | solution.py:40
  (487 shorter events, 213.5 us)
Async XLA Ops:
  7.2 74.1 %copy-start = (bf16[1,768,768]{2,1,0:T(8,128)(2,1)S(1)}, bf16[1,768,768]{2,1,0:T(8,128)(2,1)}, u32[]{:S(2)}) copy-start(bf16[1,768,768]{2,1,0:T(8,128)(2,1)} %param.25) | copy-start | bytes 3538948
  7.2 70.9 %all-reduce.16.cloned.1.call-start = ((), (), s32[]{:S(2)}) async-start(), calls=%async_computation | async-start | bytes 1966080 | tf_op jit(solution)/shard_map/psum | solution.py:44
  10.7 280.1 %copy-start.103 = (f32[768]{0:T(1024)}, f32[768]{0:T(1024)S(1)}, u32[]{:S(2)}) copy-start(f32[768]{0:T(1024)S(1)} %reduce.8) | copy-start | bytes 9220
  31.9 103.6 %all-reduce.18.cloned.1.call-start = ((), (), s32[]{:S(2)}) async-start(), calls=%async_computation.1 | async-start | bytes 1966080 | tf_op jit(solution)/shard_map/psum | solution.py:44
  32.4 322.2 %copy-start.105 = (f32[768]{0:T(1024)}, f32[768]{0:T(1024)S(1)}, u32[]{:S(2)}) copy-start(f32[768]{0:T(1024)S(1)} %reduce.14) | copy-start | bytes 9220
  90.9 120.0 %all-reduce.20.cloned.1.call-start = ((), (), s32[]{:S(2)}) async-start(), calls=%async_computation.2 | async-start | bytes 1966080 | tf_op jit(solution)/shard_map/psum | solution.py:44
  136.7 8.3 collective-permute-start
  164.9 103.5 %all-reduce.22.cloned.1.call-start = ((), (), s32[]{:S(2)}) async-start(), calls=%async_computation.3 | async-start | bytes 1966080 | tf_op jit(solution)/shard_map/psum | solution.py:44
  223.7 121.5 %all-reduce.24.cloned.1.call-start = ((), (), s32[]{:S(2)}) async-start(), calls=%async_computation.4 | async-start | bytes 1966080 | tf_op jit(solution)/shard_map/psum | solution.py:44
  270.2 8.6 collective-permute-start.1
  298.3 105.9 %all-reduce.26.cloned.1.call-start = ((), (), s32[]{:S(2)}) async-start(), calls=%async_computation.5 | async-start | bytes 1966080 | tf_op jit(solution)/shard_map/psum | solution.py:44
  359.6 107.3 %all-reduce.28.cloned.1.call-start = ((), (), s32[]{:S(2)}) async-start(), calls=%async_computation.6 | async-start | bytes 1966080 | tf_op jit(solution)/shard_map/psum | solution.py:44
  422.3 122.9 %all-reduce.30.cloned.1.call-start = ((), (), s32[]{:S(2)}) async-start(), calls=%async_computation.7 | async-start | bytes 1966080 | tf_op jit(solution)/shard_map/psum | solution.py:44
  469.2 24.1 %copy-start.106 = (f32[768]{0:T(1024)S(1)}, f32[768]{0:T(1024)}, u32[]{:S(2)}) copy-start(f32[768]{0:T(1024)} %copy-done.105) | copy-start | bytes 9220
  471.3 10.4 %collective-permute-start.2 = (bf16[577,192]{0,1:T(8,128)(2,1)}, bf16[577,192]{0,1:T(8,128)(2,1)}, u32[]{:S(2)}, u32[]{:S(2)}) collective-permute-start(bf16[577,192]{0,1:T(8,128)(2,1)} %get-tuple-element.62), channel_id=1, source_target_pairs={{64,0},{65,1},{66,2},{67,3},{68,4},{69,5},{70,6},{71,7},{72,8},{73... | collective-permute-start | bytes 664712 | tf_op jit(solution)/shard_map/ppermute | solution.py:17
  500.8 107.8 %all-reduce.32.cloned.1.call-start = ((), (), s32[]{:S(2)}) async-start(), calls=%async_computation.8 | async-start | bytes 1966080 | tf_op jit(solution)/shard_map/psum | solution.py:44
  564.0 120.0 %all-reduce.34.cloned.1.call-start = ((), (), s32[]{:S(2)}) async-start(), calls=%async_computation.9 | async-start | bytes 1966080 | tf_op jit(solution)/shard_map/psum | solution.py:44
  612.8 10.1 %collective-permute-start.3 = (bf16[577,192]{0,1:T(8,128)(2,1)S(1)}, bf16[577,192]{0,1:T(8,128)(2,1)S(1)}, u32[]{:S(2)}, u32[]{:S(2)}) collective-permute-start(bf16[577,192]{0,1:T(8,128)(2,1)S(1)} %get-tuple-element.60), channel_id=1, source_target_pairs={{64,0},{65,1},{66,2},{67,3},{68,4},{69,5},{70,6},{71,7},{72,8},{73... | collective-permute-start | bytes 664712 | tf_op jit(solution)/shard_map/ppermute | solution.py:17
  639.6 118.1 %all-reduce.38.cloned.1.call-start = ((), (), s32[]{:S(2)}) async-start(), calls=%async_computation.11 | async-start | bytes 3932160 | tf_op jit(solution)/shard_map/psum | solution.py:44
  646.5 46.7 %slice-start = ((s8[4485120]{0:T(1024)(128)(4,1)}), s8[290816]{0:T(1024)(128)(4,1)S(1)}, s32[]{:S(2)}) async-start(s8[4485120]{0:T(1024)(128)(4,1)} %bitcast.266), calls=%async_computation.12 | async-start | bytes 581632
  700.8 191.0 %all-reduce.36.cloned.1.call-start = ((), (), s32[]{:S(2)}) async-start(), calls=%async_computation.10 | async-start | bytes 14155776 | tf_op jit(solution)/shard_map/psum | solution.py:40
  759.8 78.9 %copy-start.77 = (bf16[577,192]{0,1:T(8,128)(2,1)S(1)}, bf16[577,192]{0,1:T(8,128)(2,1)}, u32[]{:S(2)}) copy-start(bf16[577,192]{0,1:T(8,128)(2,1)} %copy-done.76) | copy-start | bytes 664708
  761.5 79.2 %copy-start.74 = (f32[577,192]{0,1:T(8,128)S(1)}, f32[577,192]{0,1:T(8,128)}, u32[]{:S(2)}) copy-start(f32[577,192]{0,1:T(8,128)} %get-tuple-element.63) | copy-start | bytes 1329412
  761.5 79.2 %copy-start.75 = (f32[577,192]{0,1:T(8,128)S(1)}, f32[577,192]{0,1:T(8,128)}, u32[]{:S(2)}) copy-start(f32[577,192]{0,1:T(8,128)} %get-tuple-element.61) | copy-start | bytes 1329412
  (134 other events, 469.2 us)
Sparse Core Ops, SparseCore 0:
  32.0 45.9 all-reduce.15
  91.0 44.4 all-reduce.17
  165.0 45.8 all-reduce.19
  223.9 44.4 all-reduce.21
  298.4 46.7 all-reduce.23
  359.7 44.4 all-reduce.25
  422.4 44.4 all-reduce.27
  500.9 44.2 all-reduce.29
  564.1 44.4 all-reduce.31
  639.7 44.2 all-reduce.33
  700.9 56.7 all-reduce.37
  762.5 129.2 all-reduce.35

commit v2 on v1

--- a/solution.py
+++ b/solution.py
@@ -40,8 +40,20 @@
     return lax.psum(gradients, "dp")
 
 
+def tensor_scatter_sum(partial_value):
+    group = lax.axis_size("tensor")
+    rows_count, full_width = partial_value.shape
+    pieces = lax.all_to_all(
+        partial_value.astype(jnp.bfloat16), "tensor", 1, 0, tiled=True
+    ).reshape(group, rows_count, full_width // group)
+    return jnp.sum(pieces.astype(jnp.float32), axis=0)
+
+
 def tensor_sum(partial_value):
-    return lax.psum(partial_value.astype(jnp.bfloat16), "tensor").astype(jnp.float32)
+    summed = tensor_scatter_sum(partial_value)
+    return lax.all_gather(summed.astype(jnp.bfloat16), "tensor", axis=1, tiled=True).astype(
+        jnp.float32
+    )
 
 
 def layer_forward(partial_residual, params, column):
@@ -109,9 +121,12 @@
     )
     hidden_pre = jnp.dot(second_normalized, up_mat, preferred_element_type=jnp.float32) + up_add
     hidden = jax.nn.gelu(hidden_pre, approximate=False).astype(jnp.bfloat16)
-    feed_out = tensor_sum(jnp.dot(hidden, down_mat, preferred_element_type=jnp.float32))
-    result = middle + feed_out + down_add
-    result_part = lax.dynamic_slice_in_dim(result, column, part_width, 1)
+    feed_out = tensor_scatter_sum(jnp.dot(hidden, down_mat, preferred_element_type=jnp.float32))
+    result_part = (
+        lax.dynamic_slice_in_dim(middle, column, part_width, 1)
+        + feed_out
+        + lax.dynamic_slice_in_dim(down_add, column, part_width, 0)
+    )
     saved_state = (
         first_centered_unit,
         first_inverse_deviation,
@@ -364,7 +379,13 @@
         grads_in = grads_in + placed[:, None, None].astype(jnp.float32) * stream_grad[None]
         if step_index < micro_count:
             coming_back = shifted(stream_grad.astype(jnp.bfloat16), "section", -1)
-    grad_sums = member_sum(grad_sums)
+    flat_sums = member_sum(jnp.concatenate([gradient.reshape(-1) for gradient in grad_sums]))
+    unpacked = []
+    offset = 0
+    for gradient in grad_sums:
+        unpacked.append(flat_sums[offset : offset + gradient.size].reshape(gradient.shape))
+        offset += gradient.size
+    grad_sums = tuple(unpacked)
     return (layer_outputs[None], grads_in[None]) + tuple((gradient[None] for gradient in grad_sums))
 
 

time: 913 us -> 833 us (0.912)
  waiting for transfers between devices: 522 us -> 200 us
  local copies, waits for them, and re-layouts: 34.1 us -> 157 us
  blocking collectives: 142 us -> 211 us
  starting transfers between devices: 10.4 us -> 51.7 us
  other arithmetic: 69.1 us -> 82.1 us
    psum x11 -> x0, waiting for transfers between devices: 447 us -> none  [tensor_sum(): lax.psum(partial_value.astype(jnp.bfloat16), 'tensor').astype(jnp.float32)]
    all_gather x0 -> x9, blocking collectives: none -> 101 us  [tensor_sum(): lax.all_gather(summed.astype(jnp.bfloat16), 'tensor', axis=1, tiled=True)]
    psum x1 -> x0, blocking collectives: 75.8 us -> none  [member_sum(): return lax.psum(gradients, 'dp')]
    all_to_all x0 -> x10, waiting for transfers between devices: none -> 75.5 us  [tensor_scatter_sum(): lax.all_to_all(partial_value.astype(jnp.bfloat16), 'tensor', 1, 0, tiled=...]
    concatenate x0 -> x1, local copies, waits for them, and re-layouts: none -> 64.9 us  [shards(): jnp.concatenate([gradient.reshape(-1) for gradient in grad_sums])]
    psum x1, waiting for transfers between devices: 49.7 us -> 102 us  [member_sum(): return lax.psum(gradients, 'dp')]
    all_to_all x0 -> x10, starting transfers between devices: none -> 41.7 us  [tensor_scatter_sum(): lax.all_to_all(partial_value.astype(jnp.bfloat16), 'tensor', 1, 0, tiled=...]
    all_to_all x0 -> x2, blocking collectives: none -> 36.1 us  [tensor_scatter_sum(): lax.all_to_all(partial_value.astype(jnp.bfloat16), 'tensor', 1, 0, tiled=...]
  transfers between devices with their start and end apart: 16 -> 15, of which waited for: 16 -> 12; matrix products, arithmetic and copies ran while one was open for 6% -> 10% of each run, Pallas kernels for 0% -> 0%
where the time goes in v2:
time: 833 us; the launch traced here: 821 us
  blocking collectives  211 us (25%)
  waiting for transfers between devices  200 us (24%)
  local copies, waits for them, and re-layouts  157 us (19%)
  matrix products  99.9 us (12%)
  other arithmetic  82.1 us (10%)
  starting transfers between devices  51.7 us (6%)
  between operations  20.1 us (2%)
    psum x1, waiting for transfers between devices, member_sum(): return lax.psum(gradients, 'dp')  102 us
    all_gather x9, blocking collectives, tensor_sum(): lax.all_gather(summed.astype(jnp.bfloat16), 'tensor', axis=1, tiled=True)  101 us
    all_to_all x10, waiting for transfers between devices, tensor_scatter_sum(): lax.all_to_all(partial_value.astype(jnp.bfloat16), 'tensor', 1, 0, tiled=...  75.5 us
    concatenate x1, local copies, waits for them, and re-layouts, shards(): jnp.concatenate([gradient.reshape(-1) for gradient in grad_sums])  64.9 us
    all_gather x3, blocking collectives, layer_backward(): grad_full_bf16 = lax.all_gather(grad_part, 'tensor', axis=1, tiled=True)  41.9 us
    all_to_all x10, starting transfers between devices, tensor_scatter_sum(): lax.all_to_all(partial_value.astype(jnp.bfloat16), 'tensor', 1, 0, tiled=...  41.7 us
    all_to_all x2, blocking collectives, tensor_scatter_sum(): lax.all_to_all(partial_value.astype(jnp.bfloat16), 'tensor', 1, 0, tiled=...  36.1 us
    dot_general x12, matrix products, contract_rows(): lax.dot_general(left_side, right_side, (((0,), (0,)), ((), ())), preferre...  35.2 us
  transfers between devices with their start and end apart: 15, of which 12 were waited for; matrix products, arithmetic and copies ran while one was open for 10% of the time, Pallas kernels for 0%

profile of v2, /device:TPU:0, one launch (start us, length us, event | category | flops | bytes accessed | tf_op | source)
XLA Modules:
  0.0 821.2 jit_solution(293552219122720393)
XLA Ops:
  11.7 12.1 %all-gather = bf16[1,577,768]{1,2,0:T(8,128)(2,1)S(1)} all-gather(bf16[1,577,192]{1,2,0:T(8,128)(2,1)S(1)} %dynamic-slice_select_fusion), channel_id=2, replica_groups=mesh['section'=2,'dp'=16,'tensor'=4] {'tensor'}, dimensions={2}, use_global_device_ids=true | all-gather | bytes 1107840 | tf_op jit(solution)/shard_map/all_gather | solution.py:79
  38.4 15.2 %all-to-all-done = bf16[577,4,192]{0,2,1:T(8,128)(2,1)} async-done(((bf16[577,4,192]{0,2,1:T(8,128)(2,1)}), bf16[577,4,192]{0,2,1:T(8,128)(2,1)}, u32[]{:S(2)}, u32[]{:S(2)}) %all-to-all-start) | async-done | bytes 886304 | tf_op jit(solution)/shard_map/all_to_all | solution.py:46
  55.0 10.9 %all_gather.46 = bf16[577,768]{0,1:T(8,128)(2,1)S(1)} all-gather(bf16[577,192]{0,1:T(8,128)(2,1)S(1)} %reduce_sum.651), channel_id=1, replica_groups=mesh['section'=2,'dp'=16,'tensor'=4] {'tensor'}, dimensions={1}, use_global_device_ids=true | all-gather | bytes 1107840 | tf_op jit(solution)/shard_map/all_gather | solution.py:54
  81.9 14.5 %all-to-all-done.1 = bf16[577,4,192]{0,2,1:T(8,128)(2,1)S(1)} async-done(((bf16[577,4,192]{0,2,1:T(8,128)(2,1)}), bf16[577,4,192]{0,2,1:T(8,128)(2,1)S(1)}, u32[]{:S(2)}, u32[]{:S(2)}) %all-to-all-start.1) | async-done | bytes 886304 | tf_op jit(solution)/shard_map/all_to_all | solution.py:46
  106.5 10.0 %all_gather.47 = bf16[577,768]{0,1:T(8,128)(2,1)S(1)} all-gather(bf16[577,192]{0,1:T(8,128)(2,1)S(1)} %bitcast_select_fusion.3), channel_id=1, replica_groups=mesh['section'=2,'dp'=16,'tensor'=4] {'tensor'}, dimensions={1}, use_global_device_ids=true | all-gather | bytes 1107840 | tf_op jit(solution)/shard_map/all_gather | solution.py:79
  125.9 18.5 %all_to_all.156 = bf16[577,4,192]{0,2,1:T(8,128)(2,1)} all-to-all(bf16[577,4,192]{0,2,1:T(8,128)(2,1)S(1)} %bitcast.295), channel_id=1, replica_groups=mesh['section'=2,'dp'=16,'tensor'=4] {'tensor'}, dimensions={1} | all-to-all | bytes 1772544 | tf_op jit(solution)/shard_map/all_to_all | solution.py:46
  145.8 11.3 %all_gather.48 = bf16[577,768]{0,1:T(8,128)(2,1)S(1)} all-gather(bf16[577,192]{0,1:T(8,128)(2,1)S(1)} %reduce_sum.658), channel_id=1, replica_groups=mesh['section'=2,'dp'=16,'tensor'=4] {'tensor'}, dimensions={1}, use_global_device_ids=true | all-gather | bytes 1107840 | tf_op jit(solution)/shard_map/all_gather | solution.py:54
  170.0 17.7 %all_to_all.157 = bf16[577,4,192]{0,2,1:T(8,128)(2,1)S(1)} all-to-all(bf16[577,4,192]{0,2,1:T(8,128)(2,1)S(1)} %bitcast.296), channel_id=1, replica_groups=mesh['section'=2,'dp'=16,'tensor'=4] {'tensor'}, dimensions={1} | all-to-all | bytes 1772544 | tf_op jit(solution)/shard_map/all_to_all | solution.py:46
  199.4 10.0 %all_gather.49 = bf16[577,768]{0,1:T(8,128)(2,1)S(1)} all-gather(bf16[577,192]{0,1:T(8,128)(2,1)S(1)} %bitcast_select_fusion.2), channel_id=1, replica_groups=mesh['section'=2,'dp'=16,'tensor'=4] {'tensor'}, dimensions={1}, use_global_device_ids=true | all-gather | bytes 1107840 | tf_op jit(solution)/shard_map/all_gather | solution.py:79
  225.5 20.2 %all-gather.1 = bf16[1,577,768]{1,2,0:T(8,128)(2,1)} all-gather(bf16[1,577,192]{1,2,0:T(8,128)(2,1)S(1)} %select_select_fusion), channel_id=3, replica_groups=mesh['section'=2,'dp'=16,'tensor'=4] {'tensor'}, dimensions={2}, use_global_device_ids=true | all-gather | bytes 1107840 | tf_op jit(solution)/shard_map/all_gather | solution.py:186
  247.1 11.5 %all_gather.50 = bf16[577,768]{0,1:T(8,128)(2,1)S(1)} all-gather(bf16[577,192]{0,1:T(8,128)(2,1)S(1)} %reduce_sum.665), channel_id=1, replica_groups=mesh['section'=2,'dp'=16,'tensor'=4] {'tensor'}, dimensions={1}, use_global_device_ids=true | all-gather | bytes 1107840 | tf_op jit(solution)/shard_map/all_gather | solution.py:54
  280.3 12.7 %all-to-all-done.6 = bf16[577,4,192]{0,2,1:T(8,128)(2,1)} async-done(((bf16[577,4,192]{0,2,1:T(8,128)(2,1)}), bf16[577,4,192]{0,2,1:T(8,128)(2,1)}, u32[]{:S(2)}, u32[]{:S(2)}) %all-to-all-start.6) | async-done | bytes 886304 | tf_op jit(solution)/shard_map/all_to_all | solution.py:46
  295.1 11.4 %all_gather.52 = bf16[577,768]{0,1:T(8,128)(2,1)S(1)} all-gather(bf16[577,192]{0,1:T(8,128)(2,1)} %reduce_sum.669), channel_id=1, replica_groups=mesh['section'=2,'dp'=16,'tensor'=4] {'tensor'}, dimensions={1}, use_global_device_ids=true | all-gather | bytes 1107840 | tf_op jit(solution)/shard_map/all_gather | solution.py:54
  343.5 10.6 %all_gather.53 = bf16[577,768]{0,1:T(8,128)(2,1)S(1)} all-gather(bf16[577,192]{0,1:T(8,128)(2,1)S(1)} %reduce_sum.673), channel_id=1, replica_groups=mesh['section'=2,'dp'=16,'tensor'=4] {'tensor'}, dimensions={1}, use_global_device_ids=true | all-gather | bytes 1107840 | tf_op jit(solution)/shard_map/all_gather | solution.py:54
  368.7 10.8 %all_gather.54 = bf16[577,768]{0,1:T(8,128)(2,1)S(1)} all-gather(bf16[577,192]{0,1:T(8,128)(2,1)S(1)} %fusion.126), channel_id=1, replica_groups=mesh['section'=2,'dp'=16,'tensor'=4] {'tensor'}, dimensions={1}, use_global_device_ids=true | all-gather | bytes 1107840 | tf_op jit(solution)/shard_map/all_gather | solution.py:186
  408.4 10.9 %all_gather.55 = bf16[577,768]{0,1:T(8,128)(2,1)S(1)} all-gather(bf16[577,192]{0,1:T(8,128)(2,1)} %reduce_sum.676), channel_id=1, replica_groups=mesh['section'=2,'dp'=16,'tensor'=4] {'tensor'}, dimensions={1}, use_global_device_ids=true | all-gather | bytes 1107840 | tf_op jit(solution)/shard_map/all_gather | solution.py:54
  445.5 7.9 all-to-all-done.9
  454.8 10.6 %all_gather.56 = bf16[577,768]{0,1:T(8,128)(2,1)S(1)} all-gather(bf16[577,192]{0,1:T(8,128)(2,1)S(1)} %reduce_sum.680), channel_id=1, replica_groups=mesh['section'=2,'dp'=16,'tensor'=4] {'tensor'}, dimensions={1}, use_global_device_ids=true | all-gather | bytes 1107840 | tf_op jit(solution)/shard_map/all_gather | solution.py:54
  479.9 10.9 %all_gather.57 = bf16[577,768]{0,1:T(8,128)(2,1)S(1)} all-gather(bf16[577,192]{0,1:T(8,128)(2,1)S(1)} %fusion.125), channel_id=1, replica_groups=mesh['section'=2,'dp'=16,'tensor'=4] {'tensor'}, dimensions={1}, use_global_device_ids=true | all-gather | bytes 1107840 | tf_op jit(solution)/shard_map/all_gather | solution.py:186
  521.8 11.8 %all_gather.58 = bf16[577,768]{0,1:T(8,128)(2,1)S(1)} all-gather(bf16[577,192]{0,1:T(8,128)(2,1)} %reduce_sum.683), channel_id=1, replica_groups=mesh['section'=2,'dp'=16,'tensor'=4] {'tensor'}, dimensions={1}, use_global_device_ids=true | all-gather | bytes 1107840 | tf_op jit(solution)/shard_map/all_gather | solution.py:54
  573.4 11.8 %all_gather.59 = bf16[577,768]{0,1:T(8,128)(2,1)S(1)} all-gather(bf16[577,192]{0,1:T(8,128)(2,1)S(1)} %reduce_sum.687), channel_id=1, replica_groups=mesh['section'=2,'dp'=16,'tensor'=4] {'tensor'}, dimensions={1}, use_global_device_ids=true | all-gather | bytes 1107840 | tf_op jit(solution)/shard_map/all_gather | solution.py:54
  590.9 64.9 %concatenate.3 = f32[1771776]{0:T(1024)} concatenate(f32[192]{0:T(256)} %add_add_fusion.9, f32[192]{0:T(256)} %add_add_fusion.8, f32[442368]{0:T(1024)} %reshape.471, f32[384]{0:T(512)S(1)} %add.509, f32[147456]{0:T(1024)} %reshape.472, f32[192]{0:T(256)S(1)} %add_add_fusion.7, f32[192]{0:T(256)} %add_add_fusion.6, f32[192]{0:T(256)} %add_add_fusion.5, f32[589824]{0:T(1024)S(1)} %copy-done.30, ...), dimensions={0} | concatenate | bytes 14174208 | tf_op jit(solution)/shard_map/concatenate | solution.py:382
  666.7 13.2 %all-to-all-done.5 = bf16[577,4,192]{0,2,1:T(8,128)(2,1)S(1)} async-done(((bf16[577,4,192]{0,2,1:T(8,128)(2,1)}), bf16[577,4,192]{0,2,1:T(8,128)(2,1)S(1)}, u32[]{:S(2)}, u32[]{:S(2)}) %all-to-all-start.5) | async-done | bytes 886304 | tf_op jit(solution)/shard_map/all_to_all | solution.py:46
  683.9 102.4 %all-reduce.2.cloned.1.call-done = f32[1771776]{0:T(1024)} async-done(((f32[1771776]{0:T(1024)}), f32[1771776]{0:T(1024)}) %all-reduce.2.cloned.1.call-update) | async-done | bytes 7087120 | tf_op jit(solution)/shard_map/psum | solution.py:40
  (534 shorter events, 359.5 us)
Async XLA Ops:
  7.2 60.7 %copy-start = (bf16[1,768,768]{2,1,0:T(8,128)(2,1)S(1)}, bf16[1,768,768]{2,1,0:T(8,128)(2,1)}, u32[]{:S(2)}) copy-start(bf16[1,768,768]{2,1,0:T(8,128)(2,1)} %param.25) | copy-start | bytes 3538948
  23.9 42.0 %copy-start.4 = (bf16[1,577,768]{1,2,0:T(8,128)(2,1)}, bf16[1,577,768]{1,2,0:T(8,128)(2,1)S(1)}, u32[]{:S(2)}) copy-start(bf16[1,577,768]{1,2,0:T(8,128)(2,1)S(1)} %all-gather) | copy-start | bytes 2658820
  34.0 19.6 %all-to-all-start = ((bf16[577,4,192]{0,2,1:T(8,128)(2,1)}), bf16[577,4,192]{0,2,1:T(8,128)(2,1)}, u32[]{:S(2)}, u32[]{:S(2)}) async-start(bf16[577,4,192]{0,2,1:T(8,128)(2,1)} %bitcast.293), calls=%async_computation | async-start | bytes 1966080 | tf_op jit(solution)/shard_map/all_to_all | solution.py:46
  77.6 18.8 %all-to-all-start.1 = ((bf16[577,4,192]{0,2,1:T(8,128)(2,1)}), bf16[577,4,192]{0,2,1:T(8,128)(2,1)S(1)}, u32[]{:S(2)}, u32[]{:S(2)}) async-start(bf16[577,4,192]{0,2,1:T(8,128)(2,1)} %bitcast.15), calls=%async_computation.1 | async-start | bytes 1966080 | tf_op jit(solution)/shard_map/all_to_all | solution.py:46
  97.6 7.9 collective-permute-start
  188.9 21.0 %copy-start.80 = (bf16[577,192]{0,1:T(8,128)(2,1)}, bf16[577,192]{0,1:T(8,128)(2,1)S(1)}, u32[]{:S(2)}) copy-start(bf16[577,192]{0,1:T(8,128)(2,1)S(1)} %add_convert_fusion.12) | copy-start | bytes 664708
  188.9 9.5 %collective-permute-start.1 = (bf16[577,192]{0,1:T(8,128)(2,1)S(1)}, bf16[577,192]{0,1:T(8,128)(2,1)S(1)}, u32[]{:S(2)}, u32[]{:S(2)}) collective-permute-start(bf16[577,192]{0,1:T(8,128)(2,1)S(1)} %add_convert_fusion.12), channel_id=1, source_target_pairs={{0,64},{1,65},{2,66},{3,67},{4,68},{5,69},{6,70},{7,71},{8,72},{9,... | collective-permute-start | bytes 664712 | tf_op jit(solution)/shard_map/ppermute | solution.py:17
  219.5 26.1 %all-to-all-start.4 = ((bf16[577,4,192]{0,2,1:T(8,128)(2,1)}), bf16[577,4,192]{0,2,1:T(8,128)(2,1)}, u32[]{:S(2)}, u32[]{:S(2)}) async-start(bf16[577,4,192]{0,2,1:T(8,128)(2,1)} %bitcast.292), calls=%async_computation.4 | async-start | bytes 1966080 | tf_op jit(solution)/shard_map/all_to_all | solution.py:46
  273.4 19.6 %all-to-all-start.6 = ((bf16[577,4,192]{0,2,1:T(8,128)(2,1)}), bf16[577,4,192]{0,2,1:T(8,128)(2,1)}, u32[]{:S(2)}, u32[]{:S(2)}) async-start(bf16[577,4,192]{0,2,1:T(8,128)(2,1)} %bitcast.294), calls=%async_computation.6 | async-start | bytes 1966080 | tf_op jit(solution)/shard_map/all_to_all | solution.py:46
  277.6 34.8 %slice-start.4 = ((s8[4485120]{0:T(1024)(128)(4,1)}), s8[290816]{0:T(1024)(128)(4,1)S(1)}, s32[]{:S(2)}) async-start(s8[4485120]{0:T(1024)(128)(4,1)} %bitcast.273), calls=%async_computation.17 | async-start | bytes 581632
  322.5 19.6 %all-to-all-start.7 = ((bf16[577,4,192]{0,2,1:T(8,128)(2,1)}), bf16[577,4,192]{0,2,1:T(8,128)(2,1)}, u32[]{:S(2)}, u32[]{:S(2)}) async-start(bf16[577,4,192]{0,2,1:T(8,128)(2,1)} %bitcast.288), calls=%async_computation.7 | async-start | bytes 1966080 | tf_op jit(solution)/shard_map/all_to_all | solution.py:46
  357.5 10.2 %collective-permute-start.2 = (bf16[577,192]{0,1:T(8,128)(2,1)S(1)}, bf16[577,192]{0,1:T(8,128)(2,1)S(1)}, u32[]{:S(2)}, u32[]{:S(2)}) collective-permute-start(bf16[577,192]{0,1:T(8,128)(2,1)S(1)} %get-tuple-element.62), channel_id=1, source_target_pairs={{64,0},{65,1},{66,2},{67,3},{68,4},{69,5},{70,6},{71,7},{72,8},{73... | collective-permute-start | bytes 664712 | tf_op jit(solution)/shard_map/ppermute | solution.py:17
  358.8 20.7 %copy-start.140 = (f32[577,768]{1,0:T(8,128)S(1)}, f32[577,768]{1,0:T(8,128)}, u32[]{:S(2)}) copy-start(f32[577,768]{1,0:T(8,128)} %get-tuple-element.70) | copy-start | bytes 5317636
  358.8 20.7 %copy-start.141 = (f32[577,768]{1,0:T(8,128)S(1)}, f32[577,768]{1,0:T(8,128)}, u32[]{:S(2)}) copy-start(f32[577,768]{1,0:T(8,128)} %get-tuple-element.120) | copy-start | bytes 5317636
  386.7 19.6 %all-to-all-start.8 = ((bf16[577,4,192]{0,2,1:T(8,128)(2,1)}), bf16[577,4,192]{0,2,1:T(8,128)(2,1)}, u32[]{:S(2)}, u32[]{:S(2)}) async-start(bf16[577,4,192]{0,2,1:T(8,128)(2,1)} %bitcast.290), calls=%async_computation.8 | async-start | bytes 1966080 | tf_op jit(solution)/shard_map/all_to_all | solution.py:46
  397.6 26.2 %slice-start.2 = ((s8[4485120]{0:T(1024)(128)(4,1)}), s8[290816]{0:T(1024)(128)(4,1)S(1)}, s32[]{:S(2)}) async-start(s8[4485120]{0:T(1024)(128)(4,1)} %bitcast.271), calls=%async_computation.15 | async-start | bytes 581632
  433.8 19.6 %all-to-all-start.9 = ((bf16[577,4,192]{0,2,1:T(8,128)(2,1)}), bf16[577,4,192]{0,2,1:T(8,128)(2,1)}, u32[]{:S(2)}, u32[]{:S(2)}) async-start(bf16[577,4,192]{0,2,1:T(8,128)(2,1)} %bitcast.291), calls=%async_computation.9 | async-start | bytes 1966080 | tf_op jit(solution)/shard_map/all_to_all | solution.py:46
  468.9 10.1 %collective-permute-start.3 = (bf16[577,192]{0,1:T(8,128)(2,1)S(1)}, bf16[577,192]{0,1:T(8,128)(2,1)S(1)}, u32[]{:S(2)}, u32[]{:S(2)}) collective-permute-start(bf16[577,192]{0,1:T(8,128)(2,1)S(1)} %get-tuple-element.60), channel_id=1, source_target_pairs={{64,0},{65,1},{66,2},{67,3},{68,4},{69,5},{70,6},{71,7},{72,8},{73... | collective-permute-start | bytes 664712 | tf_op jit(solution)/shard_map/ppermute | solution.py:17
  497.5 22.1 %all-to-all-start.10 = ((bf16[577,4,192]{0,2,1:T(8,128)(2,1)}), bf16[577,4,192]{0,2,1:T(8,128)(2,1)}, u32[]{:S(2)}, u32[]{:S(2)}) async-start(bf16[577,4,192]{0,2,1:T(8,128)(2,1)} %bitcast.289), calls=%async_computation.10 | async-start | bytes 1966080 | tf_op jit(solution)/shard_map/all_to_all | solution.py:46
  514.6 23.4 %slice-start = ((s8[4485120]{0:T(1024)(128)(4,1)}), s8[290816]{0:T(1024)(128)(4,1)S(1)}, s32[]{:S(2)}) async-start(s8[4485120]{0:T(1024)(128)(4,1)} %bitcast.269), calls=%async_computation.13 | async-start | bytes 581632
  548.3 23.6 %all-to-all-start.11 = ((bf16[577,4,192]{0,2,1:T(8,128)(2,1)}), bf16[577,4,192]{0,2,1:T(8,128)(2,1)}, u32[]{:S(2)}, u32[]{:S(2)}) async-start(bf16[577,4,192]{0,2,1:T(8,128)(2,1)} %bitcast.287), calls=%async_computation.11 | async-start | bytes 1966080 | tf_op jit(solution)/shard_map/all_to_all | solution.py:46
  552.6 233.7 %all-reduce.2.cloned.1.call-start = ((), (), s32[]{:S(2)}) async-start(), calls=%async_computation.12 | async-start | bytes 14180352 | tf_op jit(solution)/shard_map/psum | solution.py:40
  660.4 20.9 %copy-start.79 = (bf16[577,192]{0,1:T(8,128)(2,1)S(1)}, bf16[577,192]{0,1:T(8,128)(2,1)}, u32[]{:S(2)}) copy-start(bf16[577,192]{0,1:T(8,128)(2,1)} %copy-done.78) | copy-start | bytes 664708
  660.4 19.6 %all-to-all-start.5 = ((bf16[577,4,192]{0,2,1:T(8,128)(2,1)}), bf16[577,4,192]{0,2,1:T(8,128)(2,1)S(1)}, u32[]{:S(2)}, u32[]{:S(2)}) async-start(bf16[577,4,192]{0,2,1:T(8,128)(2,1)} %bitcast.38), calls=%async_computation.5 | async-start | bytes 1966080 | tf_op jit(solution)/shard_map/all_to_all | solution.py:46
  (139 other events, 586.5 us)
Sparse Core Ops, SparseCore 0:
  655.9 130.3 all-reduce.1

commit v3 on v2

--- a/solution.py
+++ b/solution.py
@@ -286,6 +286,48 @@
     return (local_cols(stream_grad), attention_grads + feed_grads)
 
 
+def swap_sections(value):
+    return lax.ppermute(value, "section", [(0, 1), (1, 0)])
+
+
+def pack_small(grads):
+    (g1, b1, qkv, qv, out, ob, g2, b2, fc1, fc1b, fc2, fc2b) = grads
+    rows = jnp.stack(
+        [
+            jnp.concatenate([g1, b1, qv[0], qv[1]]),
+            jnp.concatenate([ob, g2, b2, fc2b]),
+            fc1b,
+        ]
+    )
+    return (qkv, out, fc1, jnp.concatenate([fc2, rows], axis=0))
+
+
+def unpack_small(packed, part_width):
+    qkv, out, fc1, fc2_ext = packed
+    fc2 = fc2_ext[:-3]
+    rows = fc2_ext[-3:]
+    w = part_width
+
+    def piece(row, index):
+        return rows[row, index * w : (index + 1) * w]
+
+    qv = jnp.stack([piece(0, 2), piece(0, 3)])
+    return (
+        piece(0, 0),
+        piece(0, 1),
+        qkv,
+        qv,
+        out,
+        piece(1, 0),
+        piece(1, 1),
+        piece(1, 2),
+        fc1,
+        rows[2],
+        fc2,
+        piece(1, 3),
+    )
+
+
 def shards(
     images,
     slot_table,
@@ -303,7 +345,7 @@
     fc2_bias,
     cotangent,
 ):
-    params = tuple(
+    own_params = tuple(
         (
             weight_arg[0]
             for weight_arg in (
@@ -322,70 +364,78 @@
             )
         )
     )
+    other_params = tuple(swap_sections(weight) for weight in own_params)
     section_index = lax.axis_index("section")
+    first_section = section_index == 0
+    first_params = tuple(
+        jnp.where(first_section, mine, theirs) for mine, theirs in zip(own_params, other_params)
+    )
+    second_params = tuple(
+        jnp.where(first_section, theirs, mine) for mine, theirs in zip(own_params, other_params)
+    )
     part_width = images.shape[2]
     column = lax.axis_index("tensor") * part_width
     slot_count = images.shape[0]
-    micro_count = slot_table.shape[0]
     slot_ids = jnp.arange(slot_count, dtype=jnp.int32)
 
-    def locate(batch_index):
-        clipped = jnp.clip(batch_index, 0, micro_count - 1)
-        chosen = lax.dynamic_index_in_dim(slot_table, clipped, 0, keepdims=False)
-        active = (batch_index >= 0) & (batch_index < micro_count) & (chosen < slot_count)
-        return (jnp.minimum(chosen, slot_count - 1), active, (slot_ids == chosen) & active)
-
-    received = jnp.zeros(images.shape[1:], jnp.bfloat16)
-    layer_outputs = jnp.zeros(images.shape, jnp.bfloat16)
-    saved_states = []
-    for step_index in range(micro_count + 1):
-        where_from, active, placed = locate(step_index - section_index)
-        own_image = lax.dynamic_index_in_dim(images, where_from, 0, keepdims=False)
-        entering = jnp.where(section_index == 0, own_image, received)
-        leaving, layer_state = layer_forward(entering, params, column)
-        saved_states.append(layer_state)
-        layer_outputs = layer_outputs + placed[:, None, None].astype(jnp.bfloat16) * leaving[None]
-        if step_index < micro_count:
-            received = shifted(leaving, "section", 1)
+    mine_slot = lax.dynamic_index_in_dim(slot_table, section_index, 0, keepdims=False)
+    theirs_slot = lax.dynamic_index_in_dim(slot_table, 1 - section_index, 0, keepdims=False)
+    mine_active = mine_slot < slot_count
+    theirs_active = theirs_slot < slot_count
+    mine_placed = (slot_ids == mine_slot) & mine_active
+    theirs_placed = (slot_ids == theirs_slot) & theirs_active
+    where_from = jnp.minimum(mine_slot, slot_count - 1)
+
+    own_image = lax.dynamic_index_in_dim(images, where_from, 0, keepdims=False)
+    first_out, first_state = layer_forward(own_image, first_params, column)
+    second_out, second_state = layer_forward(first_out, second_params, column)
+    kept_out = jnp.where(first_section, first_out, second_out)
+    sent_out = swap_sections(jnp.where(first_section, second_out, first_out))
+    layer_outputs = (
+        mine_placed[:, None, None].astype(jnp.bfloat16) * kept_out[None]
+        + theirs_placed[:, None, None].astype(jnp.bfloat16) * sent_out[None]
+    )
 
     def zeros_of(extent):
         return jnp.zeros(extent, jnp.float32)
 
-    grad_sums = (
-        zeros_of((part_width,)),
-        zeros_of((part_width,)),
-        zeros_of(params[2].shape),
-        zeros_of(params[3].shape),
-        zeros_of(params[4].shape),
-        zeros_of((part_width,)),
-        zeros_of((part_width,)),
-        zeros_of((part_width,)),
-        zeros_of(params[8].shape),
-        zeros_of(params[9].shape),
-        zeros_of(params[10].shape),
-        zeros_of((part_width,)),
-    )
-    coming_back = jnp.zeros(images.shape[1:], jnp.bfloat16)
-    grads_in = jnp.zeros(images.shape, jnp.float32)
-    for step_index in range(micro_count + 1):
-        where_from, active, placed = locate(micro_count - step_index - section_index)
-        own_grad = lax.dynamic_index_in_dim(cotangent, where_from, 0, keepdims=False)
-        entering = jnp.where(
-            active, jnp.where(section_index == 1, own_grad, coming_back), jnp.zeros_like(own_grad)
-        )
-        stream_grad, grad_sums = layer_backward(
-            entering, saved_states[micro_count - step_index], params, column, grad_sums
-        )
-        grads_in = grads_in + placed[:, None, None].astype(jnp.float32) * stream_grad[None]
-        if step_index < micro_count:
-            coming_back = shifted(stream_grad.astype(jnp.bfloat16), "section", -1)
-    flat_sums = member_sum(jnp.concatenate([gradient.reshape(-1) for gradient in grad_sums]))
-    unpacked = []
-    offset = 0
-    for gradient in grad_sums:
-        unpacked.append(flat_sums[offset : offset + gradient.size].reshape(gradient.shape))
-        offset += gradient.size
-    grad_sums = tuple(unpacked)
+    empty_sums = (
+        zeros_of((part_width,)),
+        zeros_of((part_width,)),
+        zeros_of(own_params[2].shape),
+        zeros_of(own_params[3].shape),
+        zeros_of(own_params[4].shape),
+        zeros_of((part_width,)),
+        zeros_of((part_width,)),
+        zeros_of((part_width,)),
+        zeros_of(own_params[8].shape),
+        zeros_of(own_params[9].shape),
+        zeros_of(own_params[10].shape),
+        zeros_of((part_width,)),
+    )
+    own_grad = lax.dynamic_index_in_dim(cotangent, where_from, 0, keepdims=False)
+    entering = jnp.where(mine_active, own_grad, jnp.zeros_like(own_grad))
+    second_dz, second_grads = layer_backward(
+        entering, second_state, second_params, column, empty_sums
+    )
+    second_sums = lax.psum(pack_small(second_grads), ("section", "dp"))
+    first_dz, first_grads = layer_backward(
+        second_dz.astype(jnp.bfloat16), first_state, first_params, column, empty_sums
+    )
+    first_packed, second_sums = lax.optimization_barrier((pack_small(first_grads), second_sums))
+    first_sums = lax.psum(first_packed, ("section", "dp"))
+    kept_dz = jnp.where(first_section, first_dz, second_dz)
+    sent_dz = swap_sections(jnp.where(first_section, second_dz, first_dz))
+    grads_in = (
+        mine_placed[:, None, None].astype(jnp.float32) * kept_dz[None]
+        + theirs_placed[:, None, None].astype(jnp.float32) * sent_dz[None]
+    )
+    grad_sums = unpack_small(
+        tuple(
+            jnp.where(first_section, early, late) for early, late in zip(first_sums, second_sums)
+        ),
+        part_width,
+    )
     return (layer_outputs[None], grads_in[None]) + tuple((gradient[None] for gradient in grad_sums))
 
 

time: 833 us -> 1070 us (1.28)
  waiting for transfers between devices: 200 us -> 667 us
  local copies, waits for them, and re-layouts: 157 us -> 43.5 us
  blocking collectives: 211 us -> 133 us
  matrix products: 99.9 us -> 76.4 us
    psum x1 -> x2, waiting for transfers between devices: 102 us -> 485 us  [the longest x1 272 us: shards(): first_sums = lax.psum(first_packed, ('section', 'dp'))]
    concatenate x1 -> x0, local copies, waits for them, and re-layouts: 64.9 us -> none  [shards(): jnp.concatenate([gradient.reshape(-1) for gradient in grad_sums])]
    all_to_all x10 -> x8, waiting for transfers between devices: 75.5 us -> 122 us  [tensor_scatter_sum(): lax.all_to_all(partial_value.astype(jnp.bfloat16), 'tensor', 1, 0, tiled=...]
    ppermute x4 -> x14, waiting for transfers between devices: 21.9 us -> 60.1 us  [swap_sections(): return lax.ppermute(value, 'section', [(0, 1), (1, 0)])]
    all_to_all x2 -> x0, blocking collectives: 36.1 us -> none  [tensor_scatter_sum(): lax.all_to_all(partial_value.astype(jnp.bfloat16), 'tensor', 1, 0, tiled=...]
    all_gather x9 -> x6, blocking collectives: 101 us -> 77.5 us  [tensor_sum(): lax.all_gather(summed.astype(jnp.bfloat16), 'tensor', axis=1, tiled=True)]
    dot_general x12 -> x8, matrix products: 35.2 us -> 21.6 us  [contract_rows(): lax.dot_general(left_side, right_side, (((0,), (0,)), ((), ())), preferre...]
    reshape x4 -> x0, local copies, waits for them, and re-layouts: 12 us -> none  [shards(): gradient.reshape(-1)]
  transfers between devices with their start and end apart: 15 -> 24, of which waited for: 12 -> 14; matrix products, arithmetic and copies ran while one was open for 10% -> 10% of each run, Pallas kernels for 0% -> 0%
where the time goes in v3:
time: 1070 us; the launch traced here: 1060 us
  waiting for transfers between devices  667 us (62%)
  blocking collectives  133 us (12%)
  matrix products  76.4 us (7%)
  other arithmetic  73.6 us (7%)
  starting transfers between devices  49.3 us (5%)
  local copies, waits for them, and re-layouts  43.5 us (4%)
  between operations  17.8 us (2%)
    psum x1, waiting for transfers between devices, shards(): first_sums = lax.psum(first_packed, ('section', 'dp'))  272 us
    psum x1, waiting for transfers between devices, shards(): second_sums = lax.psum(pack_small(second_grads), ('section', 'dp'))  213 us
    all_to_all x8, waiting for transfers between devices, tensor_scatter_sum(): lax.all_to_all(partial_value.astype(jnp.bfloat16), 'tensor', 1, 0, tiled=...  122 us
    all_gather x6, blocking collectives, tensor_sum(): lax.all_gather(summed.astype(jnp.bfloat16), 'tensor', axis=1, tiled=True)  77.5 us
    ppermute x14, waiting for transfers between devices, swap_sections(): return lax.ppermute(value, 'section', [(0, 1), (1, 0)])  60.1 us
    all_to_all x8, starting transfers between devices, tensor_scatter_sum(): lax.all_to_all(partial_value.astype(jnp.bfloat16), 'tensor', 1, 0, tiled=...  32.8 us
    all_gather x2, blocking collectives, layer_backward(): grad_full_bf16 = lax.all_gather(grad_part, 'tensor', axis=1, tiled=True)  31.8 us
    all_gather x2, blocking collectives, layer_forward(): lax.all_gather(partial_residual, 'tensor', axis=1, tiled=True)  23.7 us
  transfers between devices with their start and end apart: 24, of which 14 were waited for; matrix products, arithmetic and copies ran while one was open for 10% of the time, Pallas kernels for 0%

profile of v3, /device:TPU:0, one launch (start us, length us, event | category | flops | bytes accessed | tf_op | source)
XLA Modules:
  0.0 1061.0 jit_solution(3670997063770497828)
XLA Ops:
  18.4 11.8 %all-gather = bf16[1,577,768]{1,2,0:T(8,128)(2,1)S(1)} all-gather(bf16[1,577,192]{1,2,0:T(8,128)(2,1)S(1)} %constant_dynamic-slice_fusion), channel_id=2, replica_groups=mesh['section'=2,'dp'=16,'tensor'=4] {'tensor'}, dimensions={2}, use_global_device_ids=true | all-gather | bytes 1107840 | tf_op jit(solution)/shard_map/all_gather | solution.py:79
  34.3 18.6 %collective-permute-done.1 = f32[768]{0:T(1024)S(1)} collective-permute-done((f32[768]{0:T(1024)S(1)}, f32[768]{0:T(1024)S(1)}, u32[]{:S(2)}, u32[]{:S(2)}) %collective-permute-start.1) | collective-permute-done | bytes 3104 | tf_op jit(solution)/shard_map/ppermute | solution.py:290
  73.9 50.8 %all-to-all-done = bf16[577,4,192]{0,2,1:T(8,128)(2,1)S(1)} async-done(((bf16[577,4,192]{0,2,1:T(8,128)(2,1)}), bf16[577,4,192]{0,2,1:T(8,128)(2,1)S(1)}, u32[]{:S(2)}, u32[]{:S(2)}) %all-to-all-start) | async-done | bytes 886304 | tf_op jit(solution)/shard_map/all_to_all | solution.py:46
  125.6 10.9 %all_gather.31 = bf16[577,768]{0,1:T(8,128)(2,1)S(1)} all-gather(bf16[577,192]{0,1:T(8,128)(2,1)} %reduce_sum.435), channel_id=1, replica_groups=mesh['section'=2,'dp'=16,'tensor'=4] {'tensor'}, dimensions={1}, use_global_device_ids=true | all-gather | bytes 1107840 | tf_op jit(solution)/shard_map/all_gather | solution.py:54
  138.6 7.9 multiply_convert_fusion.3
  160.8 7.7 collective-permute-done.11
  172.6 11.9 %all_gather.32 = bf16[577,768]{0,1:T(8,128)(2,1)S(1)} all-gather(bf16[577,192]{0,1:T(8,128)(2,1)S(1)} %add_convert_fusion.9), channel_id=1, replica_groups=mesh['section'=2,'dp'=16,'tensor'=4] {'tensor'}, dimensions={1}, use_global_device_ids=true | all-gather | bytes 1107840 | tf_op jit(solution)/shard_map/all_gather | solution.py:79
  201.5 20.4 %all-gather.1 = bf16[1,577,768]{1,2,0:T(8,128)(2,1)S(1)} all-gather(bf16[1,577,192]{1,2,0:T(8,128)(2,1)S(1)} %dynamic-slice_select_fusion), channel_id=3, replica_groups=mesh['section'=2,'dp'=16,'tensor'=4] {'tensor'}, dimensions={2}, use_global_device_ids=true | all-gather | bytes 1107840 | tf_op jit(solution)/shard_map/all_gather | solution.py:186
  226.4 12.0 %all_gather.33 = bf16[577,768]{0,1:T(8,128)(2,1)S(1)} all-gather(bf16[577,192]{0,1:T(8,128)(2,1)} %reduce_sum.442), channel_id=1, replica_groups=mesh['section'=2,'dp'=16,'tensor'=4] {'tensor'}, dimensions={1}, use_global_device_ids=true | all-gather | bytes 1107840 | tf_op jit(solution)/shard_map/all_gather | solution.py:54
  241.1 7.5 multiply_convert_fusion.2
  272.9 5.5 all-to-all-done.4
  280.5 11.1 %all_gather.35 = bf16[577,768]{0,1:T(8,128)(2,1)S(1)} all-gather(bf16[577,192]{0,1:T(8,128)(2,1)} %reduce_sum.446), channel_id=1, replica_groups=mesh['section'=2,'dp'=16,'tensor'=4] {'tensor'}, dimensions={1}, use_global_device_ids=true | all-gather | bytes 1107840 | tf_op jit(solution)/shard_map/all_gather | solution.py:54
  321.8 6.7 all-to-all-done.5
  330.6 10.9 %all_gather.36 = bf16[577,768]{0,1:T(8,128)(2,1)S(1)} all-gather(bf16[577,192]{0,1:T(8,128)(2,1)} %reduce_sum.450), channel_id=1, replica_groups=mesh['section'=2,'dp'=16,'tensor'=4] {'tensor'}, dimensions={1}, use_global_device_ids=true | all-gather | bytes 1107840 | tf_op jit(solution)/shard_map/all_gather | solution.py:54
  344.6 11.4 %all_gather.37 = bf16[577,768]{0,1:T(8,128)(2,1)S(1)} all-gather(bf16[577,192]{0,1:T(8,128)(2,1)S(1)} %get-tuple-element.86), channel_id=1, replica_groups=mesh['section'=2,'dp'=16,'tensor'=4] {'tensor'}, dimensions={1}, use_global_device_ids=true | all-gather | bytes 1107840 | tf_op jit(solution)/shard_map/all_gather | solution.py:186
  383.6 16.5 %all-to-all-done.6 = bf16[577,4,192]{0,2,1:T(8,128)(2,1)} async-done(((bf16[577,4,192]{0,2,1:T(8,128)(2,1)}), bf16[577,4,192]{0,2,1:T(8,128)(2,1)}, u32[]{:S(2)}, u32[]{:S(2)}) %all-to-all-start.6) | async-done | bytes 886304 | tf_op jit(solution)/shard_map/all_to_all | solution.py:46
  401.5 16.4 %all_gather.38 = bf16[577,768]{0,1:T(8,128)(2,1)S(1)} all-gather(bf16[577,192]{0,1:T(8,128)(2,1)S(1)} %reduce_sum.453), channel_id=1, replica_groups=mesh['section'=2,'dp'=16,'tensor'=4] {'tensor'}, dimensions={1}, use_global_device_ids=true | all-gather | bytes 1107840 | tf_op jit(solution)/shard_map/all_gather | solution.py:54
  444.8 19.2 %all-to-all-done.7 = bf16[577,4,192]{0,2,1:T(8,128)(2,1)} async-done(((bf16[577,4,192]{0,2,1:T(8,128)(2,1)}), bf16[577,4,192]{0,2,1:T(8,128)(2,1)}, u32[]{:S(2)}, u32[]{:S(2)}) %all-to-all-start.7) | async-done | bytes 886304 | tf_op jit(solution)/shard_map/all_to_all | solution.py:46
  465.4 16.2 %all_gather.39 = bf16[577,768]{0,1:T(8,128)(2,1)S(1)} all-gather(bf16[577,192]{0,1:T(8,128)(2,1)S(1)} %reduce_sum.457), channel_id=1, replica_groups=mesh['section'=2,'dp'=16,'tensor'=4] {'tensor'}, dimensions={1}, use_global_device_ids=true | all-gather | bytes 1107840 | tf_op jit(solution)/shard_map/all_gather | solution.py:54
  485.9 212.9 %all-reduce.7.cloned.1.call-done = (f32[768,3,192]{0,2,1:T(8,128)}, f32[192,768]{1,0:T(8,128)}, f32[768,768]{1,0:T(8,128)}, f32[771,768]{1,0:T(8,128)}) async-done(((f32[768,3,192]{0,2,1:T(8,128)}, f32[192,768]{1,0:T(8,128)}, f32[768,768]{1,0:T(8,128)}, f32[771,768]{1,0:T(8,128)}), (f32[768,3,192]{0,2,1:T(8,128)}, f32[192,768]{1,0:T(8,128)}, f32[768,768]{1,0:T(8,128)}, ...) | async-done | bytes 7087120 | tf_op jit(solution)/shard_map/psum | solution.py:421
  709.8 23.5 %all-to-all-done.3 = bf16[577,4,192]{0,2,1:T(8,128)(2,1)S(1)} async-done(((bf16[577,4,192]{0,2,1:T(8,128)(2,1)}), bf16[577,4,192]{0,2,1:T(8,128)(2,1)S(1)}, u32[]{:S(2)}, u32[]{:S(2)}) %all-to-all-start.3) | async-done | bytes 886304 | tf_op jit(solution)/shard_map/all_to_all | solution.py:46
  738.1 11.0 %collective-permute-done.12 = bf16[577,192]{0,1:T(8,128)(2,1)S(1)} collective-permute-done((bf16[577,192]{0,1:T(8,128)(2,1)S(1)}, bf16[577,192]{0,1:T(8,128)(2,1)S(1)}, u32[]{:S(2)}, u32[]{:S(2)}) %collective-permute-start.12) | collective-permute-done | bytes 221600 | tf_op jit(solution)/shard_map/ppermute | solution.py:290
  750.2 17.9 %collective-permute-done.13 = f32[577,192]{0,1:T(8,128)S(1)} collective-permute-done((f32[577,192]{0,1:T(8,128)S(1)}, f32[577,192]{0,1:T(8,128)S(1)}, u32[]{:S(2)}, u32[]{:S(2)}) %collective-permute-start.13) | collective-permute-done | bytes 443168 | tf_op jit(solution)/shard_map/ppermute | solution.py:290
  769.5 272.3 %all-reduce.5.cloned.1.call-done = (f32[771,768]{1,0:T(8,128)}, f32[768,3,192]{0,2,1:T(8,128)}, f32[192,768]{1,0:T(8,128)}, f32[768,768]{1,0:T(8,128)}) async-done(((f32[771,768]{1,0:T(8,128)}, f32[768,3,192]{0,2,1:T(8,128)}, f32[192,768]{1,0:T(8,128)}, f32[768,768]{1,0:T(8,128)}), (f32[771,768]{1,0:T(8,128)}, f32[768,3,192]{0,2,1:T(8,128)}, f32[192,768]{1,0:T(8,128)}, ...) | async-done | bytes 7087120 | tf_op jit(solution)/shard_map/psum | solution.py:426
  (443 shorter events, 232.3 us)
Async XLA Ops:
  7.2 23.6 %collective-permute-start.3 = (f32[2,192]{1,0:T(2,128)}, f32[2,192]{1,0:T(2,128)S(1)}, u32[]{:S(2)}, u32[]{:S(2)}) collective-permute-start(f32[2,192]{1,0:T(2,128)} %bitcast.280), channel_id=1, source_target_pairs={{0,64},{64,0},{1,65},{65,1},{2,66},{66,2},{3,67},{67,3},{4,68},{68... | collective-permute-start | bytes 4616 | tf_op jit(solution)/shard_map/ppermute | solution.py:290
  10.0 21.7 %collective-permute-start.9 = (f32[768]{0:T(1024)S(1)}, f32[768]{0:T(1024)S(1)}, u32[]{:S(2)}, u32[]{:S(2)}) collective-permute-start(f32[768]{0:T(1024)S(1)} %reduce.32), channel_id=1, source_target_pairs={{0,64},{64,0},{1,65},{65,1},{2,66},{66,2},{3,67},{67,3},{4,68},{68... | collective-permute-start | bytes 9224 | tf_op jit(solution)/shard_map/ppermute | solution.py:290
  11.0 61.1 %collective-permute-start.7 = (f32[768]{0:T(1024)S(1)}, f32[768]{0:T(1024)S(1)}, u32[]{:S(2)}, u32[]{:S(2)}) collective-permute-start(f32[768]{0:T(1024)S(1)} %reduce.31), channel_id=1, source_target_pairs={{0,64},{64,0},{1,65},{65,1},{2,66},{66,2},{3,67},{67,3},{4,68},{68... | collective-permute-start | bytes 9224 | tf_op jit(solution)/shard_map/ppermute | solution.py:290
  13.6 59.1 %collective-permute-start.6 = (f32[768]{0:T(1024)S(1)}, f32[768]{0:T(1024)S(1)}, u32[]{:S(2)}, u32[]{:S(2)}) collective-permute-start(f32[768]{0:T(1024)S(1)} %reduce.30), channel_id=1, source_target_pairs={{0,64},{64,0},{1,65},{65,1},{2,66},{66,2},{3,67},{67,3},{4,68},{68... | collective-permute-start | bytes 9224 | tf_op jit(solution)/shard_map/ppermute | solution.py:290
  14.6 58.8 %collective-permute-start.5 = (f32[768]{0:T(1024)S(1)}, f32[768]{0:T(1024)S(1)}, u32[]{:S(2)}, u32[]{:S(2)}) collective-permute-start(f32[768]{0:T(1024)S(1)} %reduce.29), channel_id=1, source_target_pairs={{0,64},{64,0},{1,65},{65,1},{2,66},{66,2},{3,67},{67,3},{4,68},{68... | collective-permute-start | bytes 9224 | tf_op jit(solution)/shard_map/ppermute | solution.py:290
  30.8 26.6 %collective-permute-start.2 = (bf16[768,3,192]{0,2,1:T(8,128)(2,1)S(1)}, bf16[768,3,192]{0,2,1:T(8,128)(2,1)}, u32[]{:S(2)}, u32[]{:S(2)}) collective-permute-start(bf16[768,3,192]{0,2,1:T(8,128)(2,1)S(1)} %bitcast.282), channel_id=1, source_target_pairs={{0,64},{64,0},{1,65},{65,1},{2,66},{66,2},{3,67},{67,3},{4,68},{68... | collective-permute-start | bytes 2654216 | tf_op jit(solution)/shard_map/ppermute | solution.py:290
  31.7 21.3 %collective-permute-start.1 = (f32[768]{0:T(1024)S(1)}, f32[768]{0:T(1024)S(1)}, u32[]{:S(2)}, u32[]{:S(2)}) collective-permute-start(f32[768]{0:T(1024)S(1)} %reduce.26), channel_id=1, source_target_pairs={{0,64},{64,0},{1,65},{65,1},{2,66},{66,2},{3,67},{67,3},{4,68},{68... | collective-permute-start | bytes 9224 | tf_op jit(solution)/shard_map/ppermute | solution.py:290
  53.0 3.6 collective-permute-start
  56.6 9.9 collective-permute-start.4
  57.5 89.0 %collective-permute-start.10 = (bf16[768,768]{1,0:T(8,128)(2,1)}, bf16[768,768]{1,0:T(8,128)(2,1)}, u32[]{:S(2)}, u32[]{:S(2)}) collective-permute-start(bf16[768,768]{1,0:T(8,128)(2,1)} %bitcast.281), channel_id=1, source_target_pairs={{0,64},{64,0},{1,65},{65,1},{2,66},{66,2},{3,67},{67,3},{4,68},{68... | collective-permute-start | bytes 3538952 | tf_op jit(solution)/shard_map/ppermute | solution.py:290
  66.5 72.0 %collective-permute-start.8 = (bf16[768,768]{1,0:T(8,128)(2,1)}, bf16[768,768]{1,0:T(8,128)(2,1)}, u32[]{:S(2)}, u32[]{:S(2)}) collective-permute-start(bf16[768,768]{1,0:T(8,128)(2,1)} %bitcast.15), channel_id=1, source_target_pairs={{0,64},{64,0},{1,65},{65,1},{2,66},{66,2},{3,67},{67,3},{4,68},{68... | collective-permute-start | bytes 3538952 | tf_op jit(solution)/shard_map/ppermute | solution.py:290
  68.6 56.1 %all-to-all-start = ((bf16[577,4,192]{0,2,1:T(8,128)(2,1)}), bf16[577,4,192]{0,2,1:T(8,128)(2,1)S(1)}, u32[]{:S(2)}, u32[]{:S(2)}) async-start(bf16[577,4,192]{0,2,1:T(8,128)(2,1)} %bitcast.14), calls=%async_computation | async-start | bytes 1966080 | tf_op jit(solution)/shard_map/all_to_all | solution.py:46
  149.6 20.8 %all-to-all-start.1 = ((bf16[577,4,192]{0,2,1:T(8,128)(2,1)}), bf16[577,4,192]{0,2,1:T(8,128)(2,1)S(1)}, u32[]{:S(2)}, u32[]{:S(2)}) async-start(bf16[577,4,192]{0,2,1:T(8,128)(2,1)} %bitcast.17), calls=%async_computation.1 | async-start | bytes 1966080 | tf_op jit(solution)/shard_map/all_to_all | solution.py:46
  154.4 14.1 %collective-permute-start.11 = (f32[768]{0:T(1024)}, f32[768]{0:T(1024)}, u32[]{:S(2)}, u32[]{:S(2)}) collective-permute-start(f32[768]{0:T(1024)} %reduce.33), channel_id=1, source_target_pairs={{0,64},{64,0},{1,65},{65,1},{2,66},{66,2},{3,67},{67,3},{4,68},{68... | collective-permute-start | bytes 9224 | tf_op jit(solution)/shard_map/ppermute | solution.py:290
  196.3 28.0 %all-to-all-start.2 = ((bf16[577,4,192]{0,2,1:T(8,128)(2,1)}), bf16[577,4,192]{0,2,1:T(8,128)(2,1)}, u32[]{:S(2)}, u32[]{:S(2)}) async-start(bf16[577,4,192]{0,2,1:T(8,128)(2,1)} %bitcast.249), calls=%async_computation.2 | async-start | bytes 1966080 | tf_op jit(solution)/shard_map/all_to_all | solution.py:46
  258.8 19.6 %all-to-all-start.4 = ((bf16[577,4,192]{0,2,1:T(8,128)(2,1)}), bf16[577,4,192]{0,2,1:T(8,128)(2,1)}, u32[]{:S(2)}, u32[]{:S(2)}) async-start(bf16[577,4,192]{0,2,1:T(8,128)(2,1)} %bitcast.247), calls=%async_computation.4 | async-start | bytes 1966080 | tf_op jit(solution)/shard_map/all_to_all | solution.py:46
  308.9 19.6 %all-to-all-start.5 = ((bf16[577,4,192]{0,2,1:T(8,128)(2,1)}), bf16[577,4,192]{0,2,1:T(8,128)(2,1)}, u32[]{:S(2)}, u32[]{:S(2)}) async-start(bf16[577,4,192]{0,2,1:T(8,128)(2,1)} %bitcast.246), calls=%async_computation.5 | async-start | bytes 1966080 | tf_op jit(solution)/shard_map/all_to_all | solution.py:46
  313.2 385.6 %all-reduce.7.cloned.1.call-start = ((), (), s32[]{:S(2)}) async-start(), calls=%async_computation.9 | async-start | bytes 14204928 | tf_op jit(solution)/shard_map/psum | solution.py:421
  369.9 30.2 %all-to-all-start.6 = ((bf16[577,4,192]{0,2,1:T(8,128)(2,1)}), bf16[577,4,192]{0,2,1:T(8,128)(2,1)}, u32[]{:S(2)}, u32[]{:S(2)}) async-start(bf16[577,4,192]{0,2,1:T(8,128)(2,1)} %bitcast.248), calls=%async_computation.6 | async-start | bytes 1966080 | tf_op jit(solution)/shard_map/all_to_all | solution.py:46
  434.3 29.7 %all-to-all-start.7 = ((bf16[577,4,192]{0,2,1:T(8,128)(2,1)}), bf16[577,4,192]{0,2,1:T(8,128)(2,1)}, u32[]{:S(2)}, u32[]{:S(2)}) async-start(bf16[577,4,192]{0,2,1:T(8,128)(2,1)} %bitcast.245), calls=%async_computation.7 | async-start | bytes 1966080 | tf_op jit(solution)/shard_map/all_to_all | solution.py:46
  438.5 603.2 %all-reduce.5.cloned.1.call-start = ((), (), s32[]{:S(2)}) async-start(), calls=%async_computation.8 | async-start | bytes 14204928 | tf_op jit(solution)/shard_map/psum | solution.py:426
  703.8 29.5 %all-to-all-start.3 = ((bf16[577,4,192]{0,2,1:T(8,128)(2,1)}), bf16[577,4,192]{0,2,1:T(8,128)(2,1)S(1)}, u32[]{:S(2)}, u32[]{:S(2)}) async-start(bf16[577,4,192]{0,2,1:T(8,128)(2,1)} %bitcast.28), calls=%async_computation.3 | async-start | bytes 1966080 | tf_op jit(solution)/shard_map/all_to_all | solution.py:46
  734.7 14.5 %collective-permute-start.12 = (bf16[577,192]{0,1:T(8,128)(2,1)S(1)}, bf16[577,192]{0,1:T(8,128)(2,1)S(1)}, u32[]{:S(2)}, u32[]{:S(2)}) collective-permute-start(bf16[577,192]{0,1:T(8,128)(2,1)S(1)} %broadcast_select_fusion.25), channel_id=1, source_target_pairs={{0,64},{64,0},{1,65},{65,1},{2,66},{66,2},{3,67},{67,3},{4,68},{68... | collective-permute-start | bytes 664712 | tf_op jit(solution)/shard_map/ppermute | solution.py:290
  734.8 33.3 %collective-permute-start.13 = (f32[577,192]{0,1:T(8,128)S(1)}, f32[577,192]{0,1:T(8,128)S(1)}, u32[]{:S(2)}, u32[]{:S(2)}) collective-permute-start(f32[577,192]{0,1:T(8,128)S(1)} %broadcast_select_fusion.23), channel_id=1, source_target_pairs={{0,64},{64,0},{1,65},{65,1},{2,66},{66,2},{3,67},{67,3},{4,68},{68... | collective-permute-start | bytes 1329416 | tf_op jit(solution)/shard_map/ppermute | solution.py:290
  (123 other events, 1379.2 us)
Sparse Core Ops, SparseCore 0:
  359.2 339.5 all-reduce.6
  702.7 338.9 all-reduce.4
